TPU v7x, 1024 devices: a whole 4x8x16 slice. The times are simulated.
1024 devices in a mesh: row: 64 (over x, y, core), col: 16 (over z).
Axes of the slice: x: 4, y: 8, z: 16, core: 2. Of those that a mesh axis runs over, the one named last changes fastest.
Arguments:
- momentum: float32 [8192, 16384], P('row', 'col'), may hold values from -6 to 6
- right_factor: float32 [16384, 256], P('col'), may hold values from -0.046875 to 0.046875
Outputs:
- new_momentum: float32 [8192, 16384], P('row', 'col')
- update: float32 [8192, 16384], P('row', 'col')
All inputs are finite; a program needn't handle non-finite values.
Results may differ from a plain program's by a relative error of at most 0.0001.
Values sent between devices are 32-bit elements; how exact they have to be, the bound alone decides.
A program may use at most 32 MiB of HBM per device.

v0:
```python
import math

import jax
import jax.numpy as jnp
from jax import lax
from jax.sharding import PartitionSpec as P

ROWS = 8192
COLS = 16384
RANK = 256


def orthonormal(left_rows, gram_sum):
    lower_tri = jnp.linalg.cholesky(gram_sum)
    return jax.scipy.linalg.solve_triangular(lower_tri, left_rows.T, lower=True).T


def local(momentum, right_factor):
    highest = lax.Precision.HIGHEST
    factor_q = right_factor
    left_orth = None
    right_block = None
    left_part = jnp.dot(momentum, factor_q, precision=highest)
    left_rows = lax.psum(left_part, "col")
    gram_part = jnp.dot(left_rows.T, left_rows, precision=highest)
    gram_sum = lax.psum(gram_part, "row")
    left_orth = orthonormal(left_rows, gram_sum)
    right_piece = lax.psum_scatter(
        lax.dot_general(
            momentum,
            left_orth,
            (((0,), (0,)), ((), ())),
            precision=highest,
            preferred_element_type=jnp.float32,
        ),
        "row",
        scatter_dimension=0,
        tiled=True,
    )
    right_block = lax.all_gather(right_piece, "row", axis=0, tiled=True)
    local_squares = jnp.sum(right_block * right_block, axis=0)
    squares = lax.psum(local_squares, "col")
    factor_q = right_block / jnp.sqrt(squares + 1e-06)
    captured = lax.dot_general(
        left_orth,
        right_block,
        (((1,), (1,)), ((), ())),
        precision=highest,
        preferred_element_type=jnp.float32,
    )
    new_momentum = momentum - 0.5 * captured
    scale = math.sqrt(ROWS * COLS / RANK)
    direction = lax.dot_general(
        left_orth,
        factor_q,
        (((1,), (1,)), ((), ())),
        precision=highest,
        preferred_element_type=jnp.float32,
    )
    update = scale * direction
    return (new_momentum, update)


def solution(mesh):
    in_specs = (P("row", "col"), P("col", None))
    out_specs = (P("row", "col"), P("row", "col"))
    return jax.shard_map(local, mesh=mesh, in_specs=in_specs, out_specs=out_specs, check_vma=False)
```

profile of v0, /device:TPU:1, one launch (start us, length us, event | category | flops | bytes accessed | tf_op | source)
XLA Modules:
  0.0 729.9 jit_solution(11623422445392575574)
XLA Ops:
  7.2 1.2 copy-done
  8.4 2.3 fusion.15
  10.8 141.0 %all-reduce.4.cloned.1.call-done = f32[128,256]{1,0:T(8,128)} async-done(((f32[128,256]{1,0:T(8,128)}), f32[128,256]{1,0:T(8,128)}) %all-reduce.4.cloned.1.call-update) | async-done | bytes 131088 | tf_op jit(solution)/shard_map/psum | solution.py:24
  151.8 2.1 fusion.16
  153.9 0.0 reduce-scatter.4.cloned.1.call-start
  154.0 216.9 %all-reduce.6.cloned.1.call-done = f32[256,256]{0,1:T(8,128)} async-done(((f32[256,256]{0,1:T(8,128)}), f32[256,256]{0,1:T(8,128)}) %all-reduce.6.cloned.1.call-update) | async-done | bytes 262160 | tf_op jit(solution)/shard_map/psum | solution.py:26
  370.9 1.1 copy.7
  372.1 11.7 %cholesky.50 = f32[128,128]{1,0:T(8,128)S(1)} custom-call(f32[128,128]{1,0:T(8,128)S(1)} %cholesky.118), custom_call_target="Cholesky" | custom-call | tf_op jit(solution)/shard_map/jit(cholesky)/cholesky | solution.py:14
  383.8 9.8 %custom-call.15 = f32[1,128,128]{1,2,0:T(8,128)S(1)} custom-call(f32[1,128,128]{2,1,0:T(8,128)S(1)} %get-tuple-element.23), custom_call_target="InvertDiagBlocksLowerTriangular" | custom-call | tf_op jit(solution)/shard_map/jit(cholesky)/cholesky | solution.py:14
  393.7 0.2 constant_dynamic-update-slice_fusion.1
  393.9 0.3 convolution_subtract_fusion.1
  394.2 11.7 %cholesky.105 = f32[128,128]{1,0:T(8,128)S(1)} custom-call(f32[128,128]{1,0:T(8,128)S(1)} %convolution_subtract_fusion.1), custom_call_target="Cholesky" | custom-call | tf_op jit(solution)/shard_map/jit(cholesky)/cholesky | solution.py:14
  405.9 0.7 compare_reduce_fusion
  408.0 0.1 triangular_solve.57
  408.1 4.2 while.1
  408.2 0.6 fusion.28
  408.8 1.4 bitcast_dynamic-update-slice_fusion.2
  410.3 0.6 fusion.28
  410.9 1.4 bitcast_dynamic-update-slice_fusion.2
  412.3 19.7 %custom-call.16 = f32[2,128,128]{1,2,0:T(8,128)S(1)} custom-call(f32[2,128,128]{2,1,0:T(8,128)S(1)} %get-tuple-element.9), custom_call_target="InvertDiagBlocksLowerTriangular" | custom-call | tf_op jit(solution)/shard_map/jit(_solve_triangular)/triangular_solve | solution.py:15
  432.0 0.3 fusion.6
  432.3 0.3 convolution_subtract_fusion
  432.6 0.3 fusion.5
  432.9 1.0 convolution_bitcast_fusion
  433.9 1.3 copy.10
  435.3 0.0 all-gather.2.cloned.1.call-start
  435.3 155.9 %reduce-scatter.4.cloned.1.call-done = f32[16,256]{1,0:T(8,128)} async-done(((f32[1024,256]{1,0:T(8,128)}), f32[16,256]{1,0:T(8,128)}) %reduce-scatter.4.cloned.1.call-update) | async-done | bytes 16400 | tf_op jit(solution)/shard_map/reduce_scatter | solution.py:28
  591.2 101.2 %all-gather.2.cloned.1.call-done = f32[1024,256]{1,0:T(8,128)} async-done(((f32[16,256]{1,0:T(8,128)}), f32[1024,256]{1,0:T(8,128)}) %all-gather.2.cloned.1.call-update) | async-done | bytes 1048592 | tf_op jit(solution)/shard_map/all_gather | solution.py:40
  692.5 1.5 multiply_reduce_fusion
  693.9 25.3 %psum.23 = f32[256]{0:T(256)S(1)} all-reduce(f32[256]{0:T(256)S(1)} %multiply_reduce_fusion), channel_id=1, replica_groups=mesh['row'=64,'col'=16] {'col'}, use_global_device_ids=true, to_apply=%region_8.9 | all-reduce | flops 256 | bytes 2048 | tf_op jit(solution)/shard_map/psum | solution.py:42
  719.2 2.1 fusion
  721.3 2.0 convolution_multiply_fusion
  (26 shorter events, 0.4 us)
Async XLA Ops:
  7.2 1.2 copy-start
  7.2 144.6 %all-reduce.4.cloned.1.call-start = ((), (), s32[]{:S(2)}) async-start(), calls=%async_computation.1 | async-start | bytes 262144 | tf_op jit(solution)/shard_map/psum | solution.py:24
  10.8 360.1 %all-reduce.6.cloned.1.call-start = ((), (), s32[]{:S(2)}) async-start(), calls=%async_computation.2 | async-start | bytes 524288 | tf_op jit(solution)/shard_map/psum | solution.py:26
  153.9 437.3 %reduce-scatter.4.cloned.1.call-start = ((), (), s32[]{:S(2)}) async-start(), calls=%async_computation.4 | async-start | bytes 1064960 | tf_op jit(solution)/shard_map/reduce_scatter | solution.py:28
  370.9 1.2 copy-start.4
  408.1 23.9 %copy-start.3 = (f32[128,256]{1,0:T(8,128)S(1)}, f32[128,256]{1,0:T(8,128)}, u32[]{:S(2)}) copy-start(f32[128,256]{1,0:T(8,128)} %all-reduce.4.cloned.1.call-done) | copy-start | bytes 393220
  412.3 20.6 %copy-start.1 = (f32[128,1024]{1,0:T(8,128)S(1)}, f32[128,1024]{1,0:T(8,128)}, u32[]{:S(2)}) copy-start(f32[128,1024]{1,0:T(8,128)} %param.2) | copy-start | bytes 1572868
  435.3 257.2 %all-gather.2.cloned.1.call-start = ((), (), s32[]{:S(2)}) async-start(), calls=%async_computation.3 | async-start | bytes 1064960 | tf_op jit(solution)/shard_map/all_gather | solution.py:40
  692.5 26.8 %copy-start.2 = (f32[1024,256]{1,0:T(8,128)S(1)}, f32[1024,256]{1,0:T(8,128)}, u32[]{:S(2)}) copy-start(f32[1024,256]{1,0:T(8,128)} %all-gather.2.cloned.1.call-done) | copy-start | bytes 3145732
Sparse Core Ops, SparseCore 0:
  10.9 140.8 all-reduce.3
  156.2 214.5 all-reduce.5
  435.4 155.7 reduce-scatter.3
  595.6 96.8 all-gather.1
where the time goes:
time: 736 us; the launch traced here: 730 us
  waiting for transfers between devices  615 us (84%)
  other arithmetic  55.3 us (8%)
  blocking collectives  25.3 us (3%)
  between operations  15.3 us (2%)
  matrix products  10.8 us (1%)
  local copies, waits for them, and re-layouts  7.82 us (1%)
    psum x1, waiting for transfers between devices, local(): gram_sum = lax.psum(gram_part, 'row')  217 us
    reduce_scatter x1, waiting for transfers between devices, local(): lax.psum_scatter(lax.dot_general(momentum, left_orth, (((0,), (0,)), ((),...  156 us
    psum x1, waiting for transfers between devices, local(): left_rows = lax.psum(left_part, 'col')  141 us
    all_gather x1, waiting for transfers between devices, local(): right_block = lax.all_gather(right_piece, 'row', axis=0, tiled=True)  101 us
    another operation x6, other arithmetic, orthonormal(): lower_tri = jnp.linalg.cholesky(gram_sum)  34 us
    psum x1, blocking collectives, local(): squares = lax.psum(local_squares, 'col')  25.3 us
    another operation x3, other arithmetic, orthonormal(): jax.scipy.linalg.solve_triangular(lower_tri, left_rows.T, lower=True)  19.7 us
  transfers between devices with their start and end apart: 4, of which 4 were waited for; matrix products, arithmetic and copies ran while one was open for 0% of the time, Pallas kernels for 0%

commit v1 on v0

v1 whole, which is shorter than its diff:
```python
import functools
import math

import jax
import jax.numpy as jnp
from jax import lax
from jax.experimental import pallas as pl
from jax.experimental.pallas import tpu as pltpu
from jax.sharding import PartitionSpec as P

ROWS = 8192
COLS = 16384
RANK = 256
CORES = 2
Y_CHIPS = 8
BLOCK = 64
HIGHEST = lax.Precision.HIGHEST
MESH = pl.DeviceIdType.MESH

STAGES = (
    "left_rs",
    "left_ag",
    "gram_core",
    "gram_y",
    "gram_x",
    "gram_yag",
    "gram_cag",
    "w_core",
    "w_x",
    "w_y",
    "w_yag",
    "w_xag",
    "w_cag",
    "norm",
)


def dot(a, b, contract=((1,), (0,))):
    return lax.dot_general(
        a, b, (contract, ((), ())), precision=HIGHEST, preferred_element_type=jnp.float32
    )


def invert_cholesky_block(work):
    b = BLOCK
    groups = b // 8
    lanes = 2 * b
    rows8 = lax.broadcasted_iota(jnp.int32, (8, lanes), 0)
    a = [work[8 * g : 8 * g + 8, :] for g in range(groups)]
    pivots = [jnp.ones((8, lanes), jnp.float32) for _ in range(groups)]

    def lane(v, j):
        return jnp.broadcast_to(v[:, j : j + 1], (8, lanes))

    def sub(v, s):
        return jnp.broadcast_to(v[s : s + 1, :], (8, lanes))

    col = [lane(a[g], 0) for g in range(groups)]
    for j in range(b):
        gj, sj = divmod(j, 8)
        pivot = sub(col[gj], sj)
        inv = 1.0 / pivot
        pivots[gj] = jnp.where(rows8 == sj, pivot, pivots[gj])
        if j == b - 1:
            break
        first = (j + 1) // 8
        nxt = {g: lane(a[g], j + 1) for g in range(first, groups)}
        ahead = sub(col[first], (j + 1) % 8) * inv
        row = sub(a[gj], sj) * inv
        new_col = list(col)
        for g in range(first, groups):
            factor = col[g]
            if g == gj:
                factor = jnp.where(rows8 > sj, factor, 0.0)
            new_col[g] = nxt[g] - factor * ahead
            a[g] = a[g] - factor * row
        col = new_col
    out = [a[g] * lax.rsqrt(pivots[g]) for g in range(groups)]
    return jnp.concatenate(out, axis=0)[:, b:]


def kernel(
    sizes,
    m_hbm,
    q_hbm,
    new_hbm,
    upd_hbm,
    m_ref,
    q_ref,
    part,
    left_in,
    left,
    gram_part,
    gram_core,
    gram_half,
    gram_y,
    gram_x,
    gram,
    w_part,
    w_core,
    w_half,
    w_x,
    w_xs,
    w_y,
    w_full,
    norm_in,
    norm_out,
    work,
    right,
    new_ref,
    upd_ref,
    send,
    recv,
    local,
):
    nx, ny, nz, rows, cols, rank = sizes
    row_at = lax.axis_index("row")
    z = lax.axis_index("col")
    c = row_at % CORES
    y = (row_at // CORES) % ny
    x = row_at // (CORES * ny)
    half = rank // 2
    piece = rows // nz
    gpiece = half // ny
    xrows = half // nx
    prow = max(8, xrows // ny)
    csplit = ny * prow // xrows
    pcol = cols // csplit

    def at_z(t):
        return {"col": t}

    def at_y(t):
        return {"row": (x * ny + t) * CORES + c}

    def at_x(t):
        return {"row": (t * ny + y) * CORES + c}

    other = {"row": (x * ny + y) * CORES + (1 - c)}

    def push(stage, src, dst, target):
        s = STAGES.index(stage)
        pltpu.make_async_remote_copy(
            src_ref=src,
            dst_ref=dst,
            send_sem=send.at[s],
            recv_sem=recv.at[s],
            device_id=target,
            device_id_type=MESH,
        ).start()

    def landed(stage, ref):
        pltpu.make_async_copy(ref, ref, recv.at[STAGES.index(stage)]).wait()

    def sent(stage, ref):
        pltpu.make_async_copy(ref, ref, send.at[STAGES.index(stage)]).wait()

    def rows_of(ref, start, size):
        return ref.at[pl.ds(pl.multiple_of(start, 8), size)]

    load_m = pltpu.make_async_copy(m_hbm, m_ref, local.at[0])
    load_q = pltpu.make_async_copy(q_hbm, q_ref, local.at[1])
    load_m.start()
    load_q.start()

    def each(n, fn):
        def body(t, carry):
            fn(t)
            return carry

        lax.fori_loop(1, n, body, 0)

    barrier = pltpu.get_barrier_semaphore()

    def greet(target):
        pl.semaphore_signal(barrier, inc=1, device_id=target, device_id_type=MESH)

    each(nz, lambda t: greet(at_z((z + t) % nz)))
    each(ny, lambda t: greet(at_y((y + t) % ny)))
    each(nx, lambda t: greet(at_x((x + t) % nx)))
    greet(other)
    load_m.wait()
    load_q.wait()
    part[...] = dot(m_ref[...], q_ref[...])
    pl.semaphore_wait(barrier, nz + ny + nx - 3 + 1)

    def far_first(t, n):
        h = t // 2
        return n // 2 + h * (2 * (t % 2) - 1)

    def left_send(t):
        off = far_first(t, nz)
        to = (z + off) % nz
        push("left_rs", rows_of(part, to * piece, piece), rows_of(left_in, (off - 1) * piece, piece), at_z(to))

    each(nz, left_send)
    landed("left_rs", left_in)
    total = part[pl.ds(pl.multiple_of(z * piece, 8), piece), :]
    for t in range(nz - 1):
        total = total + left_in[t * piece : (t + 1) * piece, :]
    left[pl.ds(pl.multiple_of(z * piece, 8), piece), :] = total
    mine = rows_of(left, z * piece, piece)
    each(nz, lambda t: push("left_ag", mine, mine, at_z((z + far_first(t, nz)) % nz)))
    landed("left_ag", left_in)

    left_now = left[...]
    left_t = left_now.T
    gram_part[...] = dot(left_t, left_now)
    push("gram_core", rows_of(gram_part, (1 - c) * half, half), gram_core, other)
    w_part[...] = dot(left_t, m_ref[...])
    push("w_core", rows_of(w_part, (1 - c) * half, half), w_core, other)
    landed("gram_core", gram_core)
    gram_half[...] = gram_part[pl.ds(pl.multiple_of(c * half, 8), half), :] + gram_core[...]

    def gram_y_send(t):
        to = (y + t) % ny
        push("gram_y", rows_of(gram_half, to * gpiece, gpiece), rows_of(gram_y, (t - 1) * gpiece, gpiece), at_y(to))

    each(ny, gram_y_send)
    landed("w_core", w_core)
    w_half[...] = w_part[pl.ds(pl.multiple_of(c * half, 8), half), :] + w_core[...]
    landed("gram_y", gram_y)
    total = gram_half[pl.ds(pl.multiple_of(y * gpiece, 8), gpiece), :]
    for t in range(ny - 1):
        total = total + gram_y[t * gpiece : (t + 1) * gpiece, :]
    gram_x[pl.ds(pl.multiple_of(x * gpiece, 8), gpiece), :] = total
    mine_g = rows_of(gram_x, x * gpiece, gpiece)
    each(nx, lambda t: push("gram_x", mine_g, mine_g, at_x((x + t) % nx)))

    def w_x_send(t):
        to = (x + t) % nx
        push("w_x", rows_of(w_half, to * xrows, xrows), rows_of(w_x, (t - 1) * xrows, xrows), at_x(to))

    each(nx, w_x_send)
    landed("gram_x", gram_x.at[pl.ds(0, (nx - 1) * gpiece)])
    total = gram_x[0:gpiece, :]
    for t in range(1, nx):
        total = total + gram_x[t * gpiece : (t + 1) * gpiece, :]
    at = c * half + y * gpiece
    gram[pl.ds(pl.multiple_of(at, 8), gpiece), :] = total
    mine_a = rows_of(gram, at, gpiece)
    each(ny, lambda t: push("gram_yag", mine_a, mine_a, at_y((y + t) % ny)))
    landed("gram_yag", gram_y)
    mine_h = rows_of(gram, c * half, half)
    push("gram_cag", mine_h, mine_h, other)

    landed("w_x", w_x)
    total = w_half[pl.ds(pl.multiple_of(x * xrows, 8), xrows), :]
    for t in range(nx - 1):
        total = total + w_x[t * xrows : (t + 1) * xrows, :]
    w_xs[...] = total

    def w_piece(ref, base, k):
        return ref.at[
            pl.ds(pl.multiple_of(base + (k // csplit) * prow, 8), prow),
            pl.ds(pl.multiple_of((k % csplit) * pcol, 128), pcol),
        ]

    def w_y_send(t):
        to = (y + t) % ny
        push("w_y", w_piece(w_xs, 0, to), w_y.at[pl.ds(pl.multiple_of((t - 1) * prow, 8), prow)], at_y(to))

    each(ny, w_y_send)
    landed("gram_cag", gram_half)

    nb = rank // BLOCK
    work[...] = gram[...]
    inverse_rows = []
    eye = (
        lax.broadcasted_iota(jnp.int32, (BLOCK, BLOCK), 0) == lax.broadcasted_iota(jnp.int32, (BLOCK, BLOCK), 1)
    ).astype(jnp.float32)
    base_x = c * half + x * xrows

    def after_block(k):
        if k == 0:
            landed("w_y", w_y)
            own = w_xs[
                pl.ds(pl.multiple_of((y // csplit) * prow, 8), prow),
                pl.ds(pl.multiple_of((y % csplit) * pcol, 128), pcol),
            ]
            for t in range(ny - 1):
                own = own + w_y[t * prow : (t + 1) * prow, :]
            w_full[
                pl.ds(pl.multiple_of(base_x + (y // csplit) * prow, 8), prow),
                pl.ds(pl.multiple_of((y % csplit) * pcol, 128), pcol),
            ] = own
            mine_w = w_piece(w_full, base_x, y)
            each(ny, lambda t: push("w_yag", mine_w, mine_w, at_y((y + t) % ny)))
        if k == 1:
            landed("w_yag", w_y)
            mine_x = rows_of(w_full, base_x, xrows)
            each(nx, lambda t: push("w_xag", mine_x, mine_x, at_x((x + t) % nx)))
        if k == 2:
            landed("w_xag", w_x)
            mine_c = rows_of(w_full, c * half, half)
            push("w_cag", mine_c, mine_c, other)

    solved = []
    for k in range(nb):
        lo, hi = k * BLOCK, (k + 1) * BLOCK
        diag = work[lo:hi, lo:hi]
        inv_kk = invert_cholesky_block(jnp.concatenate([diag, eye], axis=1))
        if k == 0:
            inv_row = inv_kk
        else:
            acc = None
            for i in range(k):
                term = dot(solved[i][:, lo - (i + 1) * BLOCK : lo - i * BLOCK], inverse_rows[i], ((0,), (0,)))
                width = (i + 1) * BLOCK
                if width < lo:
                    term = jnp.concatenate([term, jnp.zeros((BLOCK, lo - width), jnp.float32)], axis=1)
                acc = term if acc is None else acc + term
            inv_row = jnp.concatenate([-dot(inv_kk, acc), inv_kk], axis=1)
        inverse_rows.append(inv_row)
        if hi < rank:
            u = dot(inv_kk, work[lo:hi, hi:])
            solved.append(u)
            work[hi:, hi:] = work[hi:, hi:] - dot(u, u, ((0,), (0,)))
        after_block(k)
    inverse = jnp.concatenate(
        [
            r if r.shape[1] == rank else jnp.concatenate([r, jnp.zeros((BLOCK, rank - r.shape[1]), jnp.float32)], axis=1)
            for r in inverse_rows
        ],
        axis=0,
    )
    left_orth = dot(left[...], inverse, ((1,), (1,)))
    landed("w_cag", w_half)
    right[...] = dot(inverse, w_full[...])
    r = right[...]
    ones = jnp.ones((8, cols), jnp.float32)
    squares = dot(ones, r * r, ((1,), (1,)))
    norm_out[...] = squares[0:1, :]
    each(nz, lambda t: push("norm", norm_out, norm_in.at[far_first(t, nz) - 1], at_z((z + far_first(t, nz)) % nz)))
    new_ref[...] = m_ref[...] - dot(0.5 * left_orth, right[...])
    store_new = pltpu.make_async_copy(new_ref, new_hbm, local.at[0])
    store_new.start()
    landed("norm", norm_in)
    total = norm_out[...]
    for t in range(nz - 1):
        total = total + norm_in[t]
    scale = math.sqrt(ROWS * COLS / RANK)
    factor = scale / jnp.sqrt(total + 1e-06)
    upd_ref[...] = dot(left_orth * factor, right[...])
    store_upd = pltpu.make_async_copy(upd_ref, upd_hbm, local.at[1])
    store_upd.start()

    sent("left_rs", left_in)
    sent("left_ag", left_in)
    sent("gram_core", gram_core)
    sent("gram_y", gram_y)
    sent("gram_x", gram_x.at[pl.ds(0, (nx - 1) * gpiece)])
    sent("gram_yag", gram_y)
    sent("gram_cag", gram_half)
    sent("w_core", w_core)
    sent("w_x", w_x)
    sent("w_y", w_y)
    sent("w_yag", w_y)
    sent("w_xag", w_x)
    sent("w_cag", w_half)
    sent("norm", norm_in)
    store_new.wait()
    store_upd.wait()


def local_step(sizes, momentum, right_factor):
    nx, ny, nz, rows, cols, rank = sizes
    half = rank // 2
    piece = rows // nz
    gpiece = half // ny
    xrows = half // nx
    prow = max(8, xrows // ny)
    pcol = cols * xrows // (ny * prow)
    f32 = jnp.float32
    vmem = lambda *shape: pltpu.VMEM(shape, f32)
    out = jax.ShapeDtypeStruct((rows, cols), f32)
    any_spec = pl.BlockSpec(memory_space=pl.ANY)
    return pl.pallas_call(
        functools.partial(kernel, sizes),
        out_shape=(out, out),
        in_specs=[any_spec, any_spec],
        out_specs=(any_spec, any_spec),
        scratch_shapes=[
            vmem(rows, cols),
            vmem(cols, rank),
            vmem(rows, rank),
            vmem(rows - piece, rank),
            vmem(rows, rank),
            vmem(rank, rank),
            vmem(half, rank),
            vmem(half, rank),
            vmem(half - gpiece, rank),
            vmem(nx * gpiece, rank),
            vmem(rank, rank),
            vmem(rank, cols),
            vmem(half, cols),
            vmem(half, cols),
            vmem(half - xrows, cols),
            vmem(xrows, cols),
            vmem((ny - 1) * prow, pcol),
            vmem(rank, cols),
            vmem(nz - 1, 1, rank),
            vmem(1, rank),
            vmem(rank, rank),
            vmem(rank, cols),
            vmem(rows, cols),
            vmem(rows, cols),
            pltpu.SemaphoreType.DMA((len(STAGES),)),
            pltpu.SemaphoreType.DMA((len(STAGES),)),
            pltpu.SemaphoreType.DMA((2,)),
        ],
        compiler_params=pltpu.CompilerParams(collective_id=0, has_side_effects=True, vmem_limit_bytes=40 * 2**20),
        name="dion",
    )(momentum, right_factor)


def solution(mesh):
    nz = mesh.shape["col"]
    ny = Y_CHIPS
    nx = mesh.shape["row"] // (ny * CORES)

    def local(momentum, right_factor):
        sizes = (nx, ny, nz, momentum.shape[0], momentum.shape[1], right_factor.shape[1])
        return local_step(sizes, momentum, right_factor)

    in_specs = (P("row", "col"), P("col", None))
    out_specs = (P("row", "col"), P("row", "col"))
    return jax.shard_map(local, mesh=mesh, in_specs=in_specs, out_specs=out_specs, check_vma=False)
```

time: 736 us -> 95.9 us (0.13)
  waiting for transfers between devices: 615 us -> 0 us
  Pallas kernels: 0 us -> 91.2 us
  other arithmetic: 55.3 us -> 0 us
  blocking collectives: 25.3 us -> 0 us
  between operations: 15.3 us -> 0.65 us
  matrix products: 10.8 us -> 0 us
    psum x2 -> x0, waiting for transfers between devices: 358 us -> none  [the longest x1 217 us: local(): gram_sum = lax.psum(gram_part, 'row')]
    reduce_scatter x1 -> x0, waiting for transfers between devices: 156 us -> none  [local(): lax.psum_scatter(lax.dot_general(momentum, left_orth, (((0,), (0,)), ((),...]
    all_gather x1 -> x0, waiting for transfers between devices: 101 us -> none  [local(): right_block = lax.all_gather(right_piece, 'row', axis=0, tiled=True)]
    pallas_call x0 -> x1, Pallas kernels: none -> 91.2 us  [local_step(): pl.pallas_call(functools.partial(kernel, sizes), out_shape=(out, out), in...]
    another operation x9 -> x0, other arithmetic: 53.7 us -> none  [the longest x6 34 us: orthonormal(): lower_tri = jnp.linalg.cholesky(gram_sum)]
    psum x1 -> x0, blocking collectives: 25.3 us -> none  [local(): squares = lax.psum(local_squares, 'col')]
    dot_general x5 -> x0, matrix products: 9.51 us -> none  [the longest x1 2.34 us: local(): left_part = jnp.dot(momentum, factor_q, precision=highest)]
  transfers between devices with their start and end apart: 4 -> 0, of which waited for: 4 -> 0; matrix products, arithmetic and copies ran while one was open for 0% -> 0% of each run, Pallas kernels for 0% -> 0%
where the time goes in v1:
time: 95.9 us; the launch traced here: 95.7 us
  Pallas kernels  91.2 us (95%)
  local copies, waits for them, and re-layouts  3.85 us (4%)
    pallas_call x1, Pallas kernels, local_step(): pl.pallas_call(functools.partial(kernel, sizes), out_shape=(out, out), in...  91.2 us
    unnamed x6, local copies, waits for them, and re-layouts  3.85 us

profile of v1, /device:TPU:1, one launch (start us, length us, event | category | flops | bytes accessed | tf_op | source)
XLA Modules:
  0.0 95.7 jit_solution(14273615525746129614)
XLA Ops:
  0.6 0.0 copy-start
  0.6 1.2 %copy-done = f32[1024,256]{1,0:T(8,128)S(1)} copy-done((f32[1024,256]{1,0:T(8,128)S(1)}, f32[1024,256]{1,0:T(8,128)}, u32[]{:S(2)}) %copy-start) | copy-done | bytes 1048600
  1.9 0.0 copy-start.1
  1.9 1.0 %copy-done.1 = f32[128,1024]{1,0:T(8,128)S(1)} copy-done((f32[128,1024]{1,0:T(8,128)S(1)}, f32[128,1024]{1,0:T(8,128)}, u32[]{:S(2)}) %copy-start.1) | copy-done | bytes 524312
  2.9 91.2 %dion.1 = (f32[128,1024]{1,0:T(8,128)S(1)}, f32[128,1024]{1,0:T(8,128)S(1)}) custom-call(f32[128,1024]{1,0:T(8,128)S(1)} %copy-done.1, f32[1024,256]{1,0:T(8,128)S(1)} %copy-done), custom_call_target="tpu_custom_call" | custom-call | tf_op jit(solution)/shard_map/dion/pallas_call | solution.py:378
  94.1 0.8 copy.6
  94.9 0.8 copy.7
Async XLA Ops:
  0.6 1.2 %copy-start = (f32[1024,256]{1,0:T(8,128)S(1)}, f32[1024,256]{1,0:T(8,128)}, u32[]{:S(2)}) copy-start(f32[1024,256]{1,0:T(8,128)} %q_hbm.1) | copy-start | bytes 3145732
  1.9 1.0 %copy-start.1 = (f32[128,1024]{1,0:T(8,128)S(1)}, f32[128,1024]{1,0:T(8,128)}, u32[]{:S(2)}) copy-start(f32[128,1024]{1,0:T(8,128)} %m_hbm.1) | copy-start | bytes 1572868

commit v2 on v1

v2 whole, which is shorter than its diff:
```python
import functools
import math

import jax
import jax.numpy as jnp
from jax import lax
from jax.experimental import pallas as pl
from jax.experimental.pallas import tpu as pltpu
from jax.sharding import PartitionSpec as P

ROWS = 8192
COLS = 16384
RANK = 256
CORES = 2
Y_CHIPS = 8
BLOCK = 64
WINDOW = 8
VMEM_BYTES = 67_000_000
HIGHEST = lax.Precision.HIGHEST
MESH = pl.DeviceIdType.MESH

STAGES = (
    "left_rs",
    "left_ag",
    "gram_core",
    "gram_y",
    "gram_x",
    "gram_yag",
    "gram_cag",
    "w_core",
    "wa_x",
    "wa_y",
    "wa_yag",
    "wa_xag",
    "wa_cag",
    "wb_y",
    "wb_x",
    "wb_xag",
    "wb_yag",
    "wb_cag",
    "norm",
)


def dot(a, b, contract=((1,), (0,))):
    return lax.dot_general(
        a, b, (contract, ((), ())), precision=HIGHEST, preferred_element_type=jnp.float32
    )


def invert_cholesky_block(work):
    b = BLOCK
    groups = b // 8
    lanes = 2 * b
    rows8 = lax.broadcasted_iota(jnp.int32, (8, lanes), 0)
    a = [work[8 * g : 8 * g + 8, :] for g in range(groups)]
    pivots = [jnp.ones((8, lanes), jnp.float32) for _ in range(groups)]

    def spread(k):
        return {g: jnp.broadcast_to(a[g][:, k : k + 1], (8, lanes)) for g in range(k // 8, groups)}

    def sub(v, s):
        return jnp.broadcast_to(v[s : s + 1, :], (8, lanes))

    window = {k: spread(k) for k in range(WINDOW)}
    for j in range(b):
        gj, sj = divmod(j, 8)
        col = window.pop(j)
        pivot = sub(col[gj], sj)
        pivots[gj] = jnp.where(rows8 == sj, pivot, pivots[gj])
        if j == b - 1:
            break
        inv = 1.0 / pivot
        factor = {g: col[g] * inv for g in range((j + 1) // 8, groups)}
        for k in range(j + 1, min(j + WINDOW, b)):
            ahead = sub(col[k // 8], k % 8)
            for g in range(k // 8, groups):
                window[k][g] = window[k][g] - factor[g] * ahead
        row = sub(a[gj], sj)
        for g in range((j + 1) // 8, groups):
            f = factor[g]
            if g == gj:
                f = jnp.where(rows8 > sj, f, 0.0)
            a[g] = a[g] - f * row
        if j + WINDOW < b:
            window[j + WINDOW] = spread(j + WINDOW)
    out = [a[g] * lax.rsqrt(pivots[g]) for g in range(groups)]
    return jnp.concatenate(out, axis=0)[:, b:]


class Plan:
    def __init__(self, nx, ny, nz, rows, cols, rank):
        self.nx, self.ny, self.nz = nx, ny, nz
        self.rows, self.cols, self.rank = rows, cols, rank
        self.half = rank // 2
        self.quarter = rank // 4
        self.piece = rows // nz
        self.gpiece = self.half // ny
        self.ax = self.quarter // nx
        self.ay_rows = max(8, self.ax // ny)
        self.ay_split = ny * self.ay_rows // self.ax
        self.ay_cols = cols // self.ay_split
        self.by = self.quarter // ny
        self.bx_cols = cols // nx


def kernel(
    p,
    m_hbm,
    q_hbm,
    new_hbm,
    upd_hbm,
    m_ref,
    q_ref,
    part,
    left_in,
    left,
    gram_part,
    gram_core,
    gram_half,
    gram_y,
    gram_x,
    gram,
    work,
    w_part,
    w_core,
    w_half,
    wa_in,
    wa_sum,
    wa_piece_in,
    wb_in,
    wb_sum,
    wb_piece_in,
    w_full,
    inverse_ref,
    right,
    norm_in,
    norm_out,
    new_ref,
    upd_ref,
    send,
    recv,
    local,
):
    nx, ny, nz, rank = p.nx, p.ny, p.nz, p.rank
    half, quarter, piece, gpiece = p.half, p.quarter, p.piece, p.gpiece
    row_at = lax.axis_index("row")
    z = lax.axis_index("col")
    c = row_at % CORES
    y = (row_at // CORES) % ny
    x = row_at // (CORES * ny)
    other = {"row": (x * ny + y) * CORES + (1 - c)}

    def at_z(t):
        return {"col": t}

    def at_y(t):
        return {"row": (x * ny + t) * CORES + c}

    def at_x(t):
        return {"row": (t * ny + y) * CORES + c}

    def push(stage, src, dst, target):
        s = STAGES.index(stage)
        pltpu.make_async_remote_copy(
            src_ref=src,
            dst_ref=dst,
            send_sem=send.at[s],
            recv_sem=recv.at[s],
            device_id=target,
            device_id_type=MESH,
        ).start()

    def landed(stage, ref):
        pltpu.make_async_copy(ref, ref, recv.at[STAGES.index(stage)]).wait()

    def sent(stage, ref):
        pltpu.make_async_copy(ref, ref, send.at[STAGES.index(stage)]).wait()

    def span(start, size, step=8):
        return pl.ds(pl.multiple_of(start, step), size)

    def rows_of(ref, start, size):
        return ref.at[span(start, size)]

    def far_first(t, n):
        h = t // 2
        return n // 2 + h * (2 * (t % 2) - 1)

    def each(n, fn):
        def body(t, carry):
            fn(far_first(t, n))
            return carry

        lax.fori_loop(1, n, body, 0)

    barrier = pltpu.get_barrier_semaphore()

    def greet(target):
        pl.semaphore_signal(barrier, inc=1, device_id=target, device_id_type=MESH)

    each(nz, lambda t: greet(at_z((z + t) % nz)))
    load_m = pltpu.make_async_copy(m_hbm, m_ref, local.at[0])
    load_q = pltpu.make_async_copy(q_hbm, q_ref, local.at[1])
    load_m.start()
    load_q.start()
    each(ny, lambda t: greet(at_y((y + t) % ny)))
    each(nx, lambda t: greet(at_x((x + t) % nx)))
    greet(other)
    load_m.wait()
    load_q.wait()
    part[...] = dot(m_ref[...], q_ref[...])
    pl.semaphore_wait(barrier, nz + ny + nx - 3 + 1)

    def left_send(t):
        to = (z + t) % nz
        push("left_rs", rows_of(part, to * piece, piece), rows_of(left_in, (t - 1) * piece, piece), at_z(to))

    each(nz, left_send)
    landed("left_rs", left_in)
    total = part[span(z * piece, piece), :]
    for t in range(nz - 1):
        total = total + left_in[t * piece : (t + 1) * piece, :]
    left[span(z * piece, piece), :] = total
    mine = rows_of(left, z * piece, piece)
    each(nz, lambda t: push("left_ag", mine, mine, at_z((z + t) % nz)))
    landed("left_ag", left_in)

    left_now = left[...]
    left_t = work.at[:, 0 : p.rows]
    left_t[...] = left_now.T
    gram_part[...] = dot(left_t[...], left_now)
    push("gram_core", rows_of(gram_part, (1 - c) * half, half), gram_core, other)
    w_part[span((1 - c) * half, half), :] = dot(left_t[span((1 - c) * half, half), :], m_ref[...])
    push("w_core", rows_of(w_part, (1 - c) * half, half), w_core, other)
    landed("gram_core", gram_core)
    gram_half[...] = gram_part[span(c * half, half), :] + gram_core[...]

    def gram_y_send(t):
        to = (y + t) % ny
        push("gram_y", rows_of(gram_half, to * gpiece, gpiece), rows_of(gram_y, (t - 1) * gpiece, gpiece), at_y(to))

    each(ny, gram_y_send)
    w_half[...] = dot(left_t[span(c * half, half), :], m_ref[...])
    landed("w_core", w_core)
    w_half[...] = w_half[...] + w_core[...]

    def wa_x_send(t):
        to = (x + t) % nx
        push("wa_x", rows_of(w_half, to * p.ax, p.ax), rows_of(wa_in, (t - 1) * p.ax, p.ax), at_x(to))

    def wb_y_send(t):
        to = (y + t) % ny
        push("wb_y", rows_of(w_half, quarter + to * p.by, p.by), rows_of(wb_in, (t - 1) * p.by, p.by), at_y(to))

    each(nx, wa_x_send)
    each(ny, wb_y_send)
    landed("gram_y", gram_y)
    total = gram_half[span(y * gpiece, gpiece), :]
    for t in range(ny - 1):
        total = total + gram_y[t * gpiece : (t + 1) * gpiece, :]
    gram_x[span(x * gpiece, gpiece), :] = total
    mine_g = rows_of(gram_x, x * gpiece, gpiece)
    each(nx, lambda t: push("gram_x", mine_g, mine_g, at_x((x + t) % nx)))
    landed("gram_x", gram_x.at[pl.ds(0, (nx - 1) * gpiece)])
    total = gram_x[0:gpiece, :]
    for t in range(1, nx):
        total = total + gram_x[t * gpiece : (t + 1) * gpiece, :]
    at = c * half + y * gpiece
    gram[span(at, gpiece), :] = total
    mine_a = rows_of(gram, at, gpiece)
    each(ny, lambda t: push("gram_yag", mine_a, mine_a, at_y((y + t) % ny)))

    def a_piece(ref, base, k):
        return ref.at[
            span(base + (k // p.ay_split) * p.ay_rows, p.ay_rows),
            span((k % p.ay_split) * p.ay_cols, p.ay_cols, 128),
        ]

    def wa_y_send(t):
        to = (y + t) % ny
        push("wa_y", a_piece(wa_sum, 0, to), rows_of(wa_piece_in, (t - 1) * p.ay_rows, p.ay_rows), at_y(to))

    landed("wa_x", wa_in)
    total = w_half[span(x * p.ax, p.ax), :]
    for t in range(nx - 1):
        total = total + wa_in[t * p.ax : (t + 1) * p.ax, :]
    wa_sum[...] = total
    each(ny, wa_y_send)

    def b_piece(ref, base, k):
        return ref.at[span(base, p.by), span(k * p.bx_cols, p.bx_cols, 128)]

    def wb_x_send(t):
        to = (x + t) % nx
        push("wb_x", b_piece(wb_sum, 0, to), rows_of(wb_piece_in, (t - 1) * p.by, p.by), at_x(to))

    landed("wb_y", wb_in)
    total = w_half[span(quarter + y * p.by, p.by), :]
    for t in range(ny - 1):
        total = total + wb_in[t * p.by : (t + 1) * p.by, :]
    wb_sum[...] = total
    each(nx, wb_x_send)

    landed("gram_yag", gram_y)
    mine_h = rows_of(gram, c * half, half)
    push("gram_cag", mine_h, mine_h, other)

    base_a = c * half + x * p.ax
    base_b = c * half + quarter + y * p.by
    landed("wb_x", wb_piece_in)
    total = b_piece(wb_sum, 0, x)[...]
    for t in range(nx - 1):
        total = total + wb_piece_in[t * p.by : (t + 1) * p.by, :]
    mine_b = b_piece(w_full, base_b, x)
    mine_b[...] = total
    each(nx, lambda t: push("wb_xag", mine_b, mine_b, at_x((x + t) % nx)))
    landed("wa_y", wa_piece_in)
    total = a_piece(wa_sum, 0, y)[...]
    for t in range(ny - 1):
        total = total + wa_piece_in[t * p.ay_rows : (t + 1) * p.ay_rows, :]
    mine_w = a_piece(w_full, base_a, y)
    mine_w[...] = total
    each(ny, lambda t: push("wa_yag", mine_w, mine_w, at_y((y + t) % ny)))
    landed("gram_cag", gram_half)

    nb = rank // BLOCK
    work[...] = gram[...]
    eye = (
        lax.broadcasted_iota(jnp.int32, (BLOCK, BLOCK), 0) == lax.broadcasted_iota(jnp.int32, (BLOCK, BLOCK), 1)
    ).astype(jnp.float32)

    def after_block(k):
        if k == 0:
            landed("wb_xag", wb_piece_in)
            rows_b = rows_of(w_full, base_b, p.by)
            each(ny, lambda t: push("wb_yag", rows_b, rows_b, at_y((y + t) % ny)))
        if k == 1:
            landed("wa_yag", wa_piece_in)
            rows_a = rows_of(w_full, base_a, p.ax)
            each(nx, lambda t: push("wa_xag", rows_a, rows_a, at_x((x + t) % nx)))

    inverse_rows = []
    solved = []
    for k in range(nb):
        lo, hi = k * BLOCK, (k + 1) * BLOCK
        diag = work[lo:hi, lo:hi]
        inv_kk = invert_cholesky_block(jnp.concatenate([diag, eye], axis=1))
        if hi < rank:
            u = dot(inv_kk, work[lo:hi, hi:])
            solved.append(u)
            work[hi:, hi:] = work[hi:, hi:] - dot(u, u, ((0,), (0,)))
        inv_row = inv_kk
        if k > 0:
            acc = None
            for i in range(k):
                term = dot(solved[i][:, lo - (i + 1) * BLOCK : lo - i * BLOCK], inverse_rows[i], ((0,), (0,)))
                width = (i + 1) * BLOCK
                if width < lo:
                    term = jnp.concatenate([term, jnp.zeros((BLOCK, lo - width), jnp.float32)], axis=1)
                acc = term if acc is None else acc + term
            inv_row = jnp.concatenate([-dot(inv_kk, acc), inv_kk], axis=1)
        inverse_rows.append(inv_row)
        if hi < rank:
            inv_row = jnp.concatenate([inv_row, jnp.zeros((BLOCK, rank - hi), jnp.float32)], axis=1)
        inverse_ref[lo:hi, :] = inv_row
        after_block(k)
    left_orth = dot(left[...], inverse_ref[...], ((1,), (1,)))
    landed("wa_xag", wa_in)
    rows_a2 = rows_of(w_full, c * half, quarter)
    push("wa_cag", rows_a2, rows_a2, other)
    landed("wb_yag", wb_in)
    rows_b2 = rows_of(w_full, c * half + quarter, quarter)
    push("wb_cag", rows_b2, rows_b2, other)
    right[...] = dot(inverse_ref[:, span(c * half, half, 128)], w_full[span(c * half, half), :])
    landed("wa_cag", w_core.at[pl.ds(0, quarter)])
    landed("wb_cag", w_core.at[pl.ds(0, quarter)])
    r = right[...] + dot(inverse_ref[:, span((1 - c) * half, half, 128)], w_full[span((1 - c) * half, half), :])
    right[...] = r
    folded = r[:, 0:128] * r[:, 0:128]
    for t in range(1, p.cols // 128):
        folded = folded + r[:, 128 * t : 128 * (t + 1)] * r[:, 128 * t : 128 * (t + 1)]
    squares = dot(jnp.ones((8, 128), jnp.float32), folded, ((1,), (1,)))
    norm_out[...] = squares[0:1, :]
    each(nz, lambda t: push("norm", norm_out, norm_in.at[t - 1], at_z((z + t) % nz)))
    new_ref[...] = m_ref[...] - dot(0.5 * left_orth, right[...])
    store_new = pltpu.make_async_copy(new_ref, new_hbm, local.at[0])
    store_new.start()
    landed("norm", norm_in)
    total = norm_out[...]
    for t in range(nz - 1):
        total = total + norm_in[t]
    scale = math.sqrt(ROWS * COLS / RANK)
    factor = scale / jnp.sqrt(total + 1e-06)
    upd_ref[...] = dot(left_orth * factor, right[...])
    store_upd = pltpu.make_async_copy(upd_ref, upd_hbm, local.at[1])
    store_upd.start()

    sent("left_rs", left_in)
    sent("left_ag", left_in)
    sent("gram_core", gram_core)
    sent("gram_y", gram_y)
    sent("gram_x", gram_x.at[pl.ds(0, (nx - 1) * gpiece)])
    sent("gram_yag", gram_y)
    sent("gram_cag", gram_half)
    sent("w_core", w_core)
    sent("wa_x", wa_in)
    sent("wa_y", wa_piece_in)
    sent("wa_yag", wa_piece_in)
    sent("wa_xag", wa_in)
    sent("wa_cag", w_core.at[pl.ds(0, quarter)])
    sent("wb_y", wb_in)
    sent("wb_x", wb_piece_in)
    sent("wb_xag", wb_piece_in)
    sent("wb_yag", wb_in)
    sent("wb_cag", w_core.at[pl.ds(0, quarter)])
    sent("norm", norm_in)
    store_new.wait()
    store_upd.wait()


def local_step(p, momentum, right_factor):
    f32 = jnp.float32
    vmem = lambda *shape: pltpu.VMEM(shape, f32)
    out = jax.ShapeDtypeStruct((p.rows, p.cols), f32)
    any_spec = pl.BlockSpec(memory_space=pl.ANY)
    return pl.pallas_call(
        functools.partial(kernel, p),
        out_shape=(out, out),
        in_specs=[any_spec, any_spec],
        out_specs=(any_spec, any_spec),
        scratch_shapes=[
            vmem(p.rows, p.cols),
            vmem(p.cols, p.rank),
            vmem(p.rows, p.rank),
            vmem(p.rows - p.piece, p.rank),
            vmem(p.rows, p.rank),
            vmem(p.rank, p.rank),
            vmem(p.half, p.rank),
            vmem(p.half, p.rank),
            vmem(p.half - p.gpiece, p.rank),
            vmem(p.nx * p.gpiece, p.rank),
            vmem(p.rank, p.rank),
            vmem(p.rank, p.rank),
            vmem(p.rank, p.cols),
            vmem(p.half, p.cols),
            vmem(p.half, p.cols),
            vmem(p.quarter - p.ax, p.cols),
            vmem(p.ax, p.cols),
            vmem((p.ny - 1) * p.ay_rows, p.ay_cols),
            vmem(p.quarter - p.by, p.cols),
            vmem(p.by, p.cols),
            vmem((p.nx - 1) * p.by, p.bx_cols),
            vmem(p.rank, p.cols),
            vmem(p.rank, p.rank),
            vmem(p.rank, p.cols),
            vmem(p.nz - 1, 1, p.rank),
            vmem(1, p.rank),
            vmem(p.rows, p.cols),
            vmem(p.rows, p.cols),
            pltpu.SemaphoreType.DMA((len(STAGES),)),
            pltpu.SemaphoreType.DMA((len(STAGES),)),
            pltpu.SemaphoreType.DMA((2,)),
        ],
        compiler_params=pltpu.CompilerParams(collective_id=0, has_side_effects=True, vmem_limit_bytes=VMEM_BYTES),
        name="dion",
    )(momentum, right_factor)


def solution(mesh):
    nz = mesh.shape["col"]
    ny = Y_CHIPS
    nx = mesh.shape["row"] // (ny * CORES)

    def local(momentum, right_factor):
        plan = Plan(nx, ny, nz, momentum.shape[0], momentum.shape[1], right_factor.shape[1])
        return local_step(plan, momentum, right_factor)

    in_specs = (P("row", "col"), P("col", None))
    out_specs = (P("row", "col"), P("row", "col"))
    return jax.shard_map(local, mesh=mesh, in_specs=in_specs, out_specs=out_specs, check_vma=False)
```

time: 95.9 us -> 85.9 us (0.90)
  Pallas kernels: 91.2 us -> 82.3 us
  local copies, waits for them, and re-layouts: 3.85 us -> 2.74 us
    pallas_call x1, Pallas kernels: 91.2 us -> 82.3 us  [local_step(): pl.pallas_call(functools.partial(kernel, p), out_shape=(out, out), in_spe...]
    unnamed x6 -> x4, local copies, waits for them, and re-layouts: 3.85 us -> 2.74 us
where the time goes in v2:
time: 85.9 us; the launch traced here: 85.7 us
  Pallas kernels  82.3 us (96%)
  local copies, waits for them, and re-layouts  2.74 us (3%)
    pallas_call x1, Pallas kernels, local_step(): pl.pallas_call(functools.partial(kernel, p), out_shape=(out, out), in_spe...  82.3 us
    unnamed x4, local copies, waits for them, and re-layouts  2.74 us

profile of v2, /device:TPU:1, one launch (start us, length us, event | category | flops | bytes accessed | tf_op | source)
XLA Modules:
  0.0 85.7 jit_solution(2983341424164846424)
XLA Ops:
  0.6 82.3 %dion.1 = (f32[128,1024]{1,0:T(8,128)}, f32[128,1024]{1,0:T(8,128)}) custom-call(f32[128,1024]{1,0:T(8,128)} %m_hbm.1, f32[1024,256]{1,0:T(8,128)} %q_hbm.1), custom_call_target="tpu_custom_call" | custom-call | tf_op jit(solution)/shard_map/dion/pallas_call | solution.py:427
  82.9 0.0 copy-start
  82.9 1.9 %copy.6 = f32[128,1024]{1,0:T(8,128)} copy(f32[128,1024]{1,0:T(8,128)} %get-tuple-element.4) | data formatting | bytes 1048576
  84.9 0.0 copy-done
  84.9 0.8 copy.7
Async XLA Ops:
  82.9 2.0 %copy-start = (f32[128,1024]{1,0:T(8,128)S(1)}, f32[128,1024]{1,0:T(8,128)}, u32[]{:S(2)}) copy-start(f32[128,1024]{1,0:T(8,128)} %get-tuple-element.5) | copy-start | bytes 1572868

commit v3 on v2

--- a/solution.py
+++ b/solution.py
@@ -15,7 +15,7 @@
 Y_CHIPS = 8
 BLOCK = 64
 WINDOW = 8
-VMEM_BYTES = 67_000_000
+VMEM_BYTES = 24 * 2**20
 HIGHEST = lax.Precision.HIGHEST
 MESH = pl.DeviceIdType.MESH
 
@@ -32,12 +32,11 @@
     "wa_y",
     "wa_yag",
     "wa_xag",
-    "wa_cag",
     "wb_y",
     "wb_x",
     "wb_xag",
     "wb_yag",
-    "wb_cag",
+    "right_core",
     "norm",
 )
 
@@ -93,23 +92,26 @@
         self.nx, self.ny, self.nz = nx, ny, nz
         self.rows, self.cols, self.rank = rows, cols, rank
         self.half = rank // 2
-        self.quarter = rank // 4
+        self.hcols = cols // 2
         self.piece = rows // nz
         self.gpiece = self.half // ny
-        self.ax = self.quarter // nx
+        self.ax = self.half // nx
         self.ay_rows = max(8, self.ax // ny)
         self.ay_split = ny * self.ay_rows // self.ax
-        self.ay_cols = cols // self.ay_split
-        self.by = self.quarter // ny
-        self.bx_cols = cols // nx
+        self.ay_cols = self.hcols // self.ay_split
+        self.by = self.half // ny
+        self.bx_rows = max(8, self.by // nx)
+        self.bx_split = nx * self.bx_rows // self.by
+        self.bx_cols = self.hcols // self.bx_split
 
 
 def kernel(
     p,
     m_hbm,
     q_hbm,
-    new_hbm,
-    upd_hbm,
+    new_out,
+    right_out,
+    left_out,
     m_ref,
     q_ref,
     part,
@@ -136,23 +138,25 @@
     right,
     norm_in,
     norm_out,
-    new_ref,
-    upd_ref,
     send,
     recv,
     local,
 ):
     nx, ny, nz, rank = p.nx, p.ny, p.nz, p.rank
-    half, quarter, piece, gpiece = p.half, p.quarter, p.piece, p.gpiece
+    half, hcols, piece, gpiece = p.half, p.hcols, p.piece, p.gpiece
     row_at = lax.axis_index("row")
     z = lax.axis_index("col")
     c = row_at % CORES
     y = (row_at // CORES) % ny
     x = row_at // (CORES * ny)
-    other = {"row": (x * ny + y) * CORES + (1 - c)}
+    other_row = (x * ny + y) * CORES + (1 - c)
+    other = {"row": other_row}
 
     def at_z(t):
         return {"col": t}
+
+    def at_z_other(t):
+        return {"row": other_row, "col": t}
 
     def at_y(t):
         return {"row": (x * ny + t) * CORES + c}
@@ -206,11 +210,12 @@
     load_q.start()
     each(ny, lambda t: greet(at_y((y + t) % ny)))
     each(nx, lambda t: greet(at_x((x + t) % nx)))
+    each(nz, lambda t: greet(at_z_other((z + t) % nz)))
     greet(other)
     load_m.wait()
     load_q.wait()
     part[...] = dot(m_ref[...], q_ref[...])
-    pl.semaphore_wait(barrier, nz + ny + nx - 3 + 1)
+    pl.semaphore_wait(barrier, 2 * nz + ny + nx - 3)
 
     def left_send(t):
         to = (z + t) % nz
@@ -231,8 +236,8 @@
     left_t[...] = left_now.T
     gram_part[...] = dot(left_t[...], left_now)
     push("gram_core", rows_of(gram_part, (1 - c) * half, half), gram_core, other)
-    w_part[span((1 - c) * half, half), :] = dot(left_t[span((1 - c) * half, half), :], m_ref[...])
-    push("w_core", rows_of(w_part, (1 - c) * half, half), w_core, other)
+    w_part[...] = dot(left_t[...], m_ref[:, span((1 - c) * hcols, hcols, 128)])
+    push("w_core", w_part, w_core, other)
     landed("gram_core", gram_core)
     gram_half[...] = gram_part[span(c * half, half), :] + gram_core[...]
 
@@ -241,7 +246,7 @@
         push("gram_y", rows_of(gram_half, to * gpiece, gpiece), rows_of(gram_y, (t - 1) * gpiece, gpiece), at_y(to))
 
     each(ny, gram_y_send)
-    w_half[...] = dot(left_t[span(c * half, half), :], m_ref[...])
+    w_half[...] = dot(left_t[...], m_ref[:, span(c * hcols, hcols, 128)])
     landed("w_core", w_core)
     w_half[...] = w_half[...] + w_core[...]
 
@@ -251,7 +256,7 @@
 
     def wb_y_send(t):
         to = (y + t) % ny
-        push("wb_y", rows_of(w_half, quarter + to * p.by, p.by), rows_of(wb_in, (t - 1) * p.by, p.by), at_y(to))
+        push("wb_y", rows_of(w_half, half + to * p.by, p.by), rows_of(wb_in, (t - 1) * p.by, p.by), at_y(to))
 
     each(nx, wa_x_send)
     each(ny, wb_y_send)
@@ -277,6 +282,12 @@
             span((k % p.ay_split) * p.ay_cols, p.ay_cols, 128),
         ]
 
+    def b_piece(ref, base, k):
+        return ref.at[
+            span(base + (k // p.bx_split) * p.bx_rows, p.bx_rows),
+            span((k % p.bx_split) * p.bx_cols, p.bx_cols, 128),
+        ]
+
     def wa_y_send(t):
         to = (y + t) % ny
         push("wa_y", a_piece(wa_sum, 0, to), rows_of(wa_piece_in, (t - 1) * p.ay_rows, p.ay_rows), at_y(to))
@@ -288,15 +299,12 @@
     wa_sum[...] = total
     each(ny, wa_y_send)
 
-    def b_piece(ref, base, k):
-        return ref.at[span(base, p.by), span(k * p.bx_cols, p.bx_cols, 128)]
-
     def wb_x_send(t):
         to = (x + t) % nx
-        push("wb_x", b_piece(wb_sum, 0, to), rows_of(wb_piece_in, (t - 1) * p.by, p.by), at_x(to))
+        push("wb_x", b_piece(wb_sum, 0, to), rows_of(wb_piece_in, (t - 1) * p.bx_rows, p.bx_rows), at_x(to))
 
     landed("wb_y", wb_in)
-    total = w_half[span(quarter + y * p.by, p.by), :]
+    total = w_half[span(half + y * p.by, p.by), :]
     for t in range(ny - 1):
         total = total + wb_in[t * p.by : (t + 1) * p.by, :]
     wb_sum[...] = total
@@ -306,12 +314,12 @@
     mine_h = rows_of(gram, c * half, half)
     push("gram_cag", mine_h, mine_h, other)
 
-    base_a = c * half + x * p.ax
-    base_b = c * half + quarter + y * p.by
+    base_a = x * p.ax
+    base_b = half + y * p.by
     landed("wb_x", wb_piece_in)
     total = b_piece(wb_sum, 0, x)[...]
     for t in range(nx - 1):
-        total = total + wb_piece_in[t * p.by : (t + 1) * p.by, :]
+        total = total + wb_piece_in[t * p.bx_rows : (t + 1) * p.bx_rows, :]
     mine_b = b_piece(w_full, base_b, x)
     mine_b[...] = total
     each(nx, lambda t: push("wb_xag", mine_b, mine_b, at_x((x + t) % nx)))
@@ -367,34 +375,36 @@
         after_block(k)
     left_orth = dot(left[...], inverse_ref[...], ((1,), (1,)))
     landed("wa_xag", wa_in)
-    rows_a2 = rows_of(w_full, c * half, quarter)
-    push("wa_cag", rows_a2, rows_a2, other)
     landed("wb_yag", wb_in)
-    rows_b2 = rows_of(w_full, c * half + quarter, quarter)
-    push("wb_cag", rows_b2, rows_b2, other)
-    right[...] = dot(inverse_ref[:, span(c * half, half, 128)], w_full[span(c * half, half), :])
-    landed("wa_cag", w_core.at[pl.ds(0, quarter)])
-    landed("wb_cag", w_core.at[pl.ds(0, quarter)])
-    r = right[...] + dot(inverse_ref[:, span((1 - c) * half, half, 128)], w_full[span((1 - c) * half, half), :])
-    right[...] = r
+    r = dot(inverse_ref[...], w_full[...])
+    right[c] = r
+    push("right_core", right.at[c], right.at[c], other)
     folded = r[:, 0:128] * r[:, 0:128]
-    for t in range(1, p.cols // 128):
+    for t in range(1, hcols // 128):
         folded = folded + r[:, 128 * t : 128 * (t + 1)] * r[:, 128 * t : 128 * (t + 1)]
     squares = dot(jnp.ones((8, 128), jnp.float32), folded, ((1,), (1,)))
     norm_out[...] = squares[0:1, :]
-    each(nz, lambda t: push("norm", norm_out, norm_in.at[t - 1], at_z((z + t) % nz)))
-    new_ref[...] = m_ref[...] - dot(0.5 * left_orth, right[...])
-    store_new = pltpu.make_async_copy(new_ref, new_hbm, local.at[0])
-    store_new.start()
+
+    def norm_send(t):
+        to = (z + t) % nz
+        push("norm", norm_out, norm_in.at[t - 1], at_z(to))
+        push("norm", norm_out, norm_in.at[nz - 1 + t], at_z_other(to))
+
+    each(nz, norm_send)
+    push("norm", norm_out, norm_in.at[nz - 1], other)
+    half_orth = 0.5 * left_orth
+    mine_cols = span(c * hcols, hcols, 128)
+    new_out[:, mine_cols] = m_ref[:, mine_cols] - dot(half_orth, right[c])
+    landed("right_core", w_half)
+    other_cols = span((1 - c) * hcols, hcols, 128)
+    new_out[:, other_cols] = m_ref[:, other_cols] - dot(half_orth, right[1 - c])
+    right_out[...] = right[...]
     landed("norm", norm_in)
     total = norm_out[...]
-    for t in range(nz - 1):
+    for t in range(2 * nz - 1):
         total = total + norm_in[t]
     scale = math.sqrt(ROWS * COLS / RANK)
-    factor = scale / jnp.sqrt(total + 1e-06)
-    upd_ref[...] = dot(left_orth * factor, right[...])
-    store_upd = pltpu.make_async_copy(upd_ref, upd_hbm, local.at[1])
-    store_upd.start()
+    left_out[...] = left_orth * (scale / jnp.sqrt(total + 1e-06))
 
     sent("left_rs", left_in)
     sent("left_ag", left_in)
@@ -408,27 +418,39 @@
     sent("wa_y", wa_piece_in)
     sent("wa_yag", wa_piece_in)
     sent("wa_xag", wa_in)
-    sent("wa_cag", w_core.at[pl.ds(0, quarter)])
     sent("wb_y", wb_in)
     sent("wb_x", wb_piece_in)
     sent("wb_xag", wb_piece_in)
     sent("wb_yag", wb_in)
-    sent("wb_cag", w_core.at[pl.ds(0, quarter)])
+    sent("right_core", w_half)
     sent("norm", norm_in)
-    store_new.wait()
-    store_upd.wait()
+
+
+def write_outputs(new_ref, right_ref, left_ref, new_hbm, upd_hbm, upd, sems):
+    hcols = right_ref.shape[2]
+    copies = [pltpu.make_async_copy(new_ref, new_hbm, sems.at[0])]
+    copies[0].start()
+    for h in range(2):
+        at = pl.ds(h * hcols, hcols)
+        upd[:, at] = dot(left_ref[...], right_ref[h])
+        copies.append(pltpu.make_async_copy(upd.at[:, at], upd_hbm.at[:, at], sems.at[1 + h]))
+        copies[-1].start()
+    for copy in copies:
+        copy.wait()
 
 
 def local_step(p, momentum, right_factor):
     f32 = jnp.float32
     vmem = lambda *shape: pltpu.VMEM(shape, f32)
-    out = jax.ShapeDtypeStruct((p.rows, p.cols), f32)
+    shaped = lambda *shape: jax.ShapeDtypeStruct(shape, f32)
     any_spec = pl.BlockSpec(memory_space=pl.ANY)
-    return pl.pallas_call(
+    hbm_spec = pl.BlockSpec(memory_space=pltpu.HBM)
+    vmem_spec = pl.BlockSpec(memory_space=pltpu.VMEM)
+    new, right, left = pl.pallas_call(
         functools.partial(kernel, p),
-        out_shape=(out, out),
-        in_specs=[any_spec, any_spec],
-        out_specs=(any_spec, any_spec),
+        out_shape=(shaped(p.rows, p.cols), shaped(2, p.rank, p.hcols), shaped(p.rows, p.rank)),
+        in_specs=[hbm_spec, hbm_spec],
+        out_specs=(vmem_spec,) * 3,
         scratch_shapes=[
             vmem(p.rows, p.cols),
             vmem(p.cols, p.rank),
@@ -442,29 +464,39 @@
             vmem(p.nx * p.gpiece, p.rank),
             vmem(p.rank, p.rank),
             vmem(p.rank, p.rank),
-            vmem(p.rank, p.cols),
-            vmem(p.half, p.cols),
-            vmem(p.half, p.cols),
-            vmem(p.quarter - p.ax, p.cols),
-            vmem(p.ax, p.cols),
+            vmem(p.rank, p.hcols),
+            vmem(p.rank, p.hcols),
+            vmem(p.rank, p.hcols),
+            vmem(p.half - p.ax, p.hcols),
+            vmem(p.ax, p.hcols),
             vmem((p.ny - 1) * p.ay_rows, p.ay_cols),
-            vmem(p.quarter - p.by, p.cols),
-            vmem(p.by, p.cols),
-            vmem((p.nx - 1) * p.by, p.bx_cols),
-            vmem(p.rank, p.cols),
+            vmem(p.half - p.by, p.hcols),
+            vmem(p.by, p.hcols),
+            vmem((p.nx - 1) * p.bx_rows, p.bx_cols),
+            vmem(p.rank, p.hcols),
             vmem(p.rank, p.rank),
-            vmem(p.rank, p.cols),
-            vmem(p.nz - 1, 1, p.rank),
+            vmem(2, p.rank, p.hcols),
+            vmem(2 * p.nz - 1, 1, p.rank),
             vmem(1, p.rank),
-            vmem(p.rows, p.cols),
-            vmem(p.rows, p.cols),
             pltpu.SemaphoreType.DMA((len(STAGES),)),
             pltpu.SemaphoreType.DMA((len(STAGES),)),
             pltpu.SemaphoreType.DMA((2,)),
         ],
         compiler_params=pltpu.CompilerParams(collective_id=0, has_side_effects=True, vmem_limit_bytes=VMEM_BYTES),
         name="dion",
-    )(momentum, right_factor)
+    )(
+        pltpu.with_memory_space_constraint(momentum, pltpu.HBM),
+        pltpu.with_memory_space_constraint(right_factor, pltpu.HBM),
+    )
+    return pl.pallas_call(
+        write_outputs,
+        out_shape=(shaped(p.rows, p.cols),) * 2,
+        in_specs=[vmem_spec] * 3,
+        out_specs=(any_spec, any_spec),
+        scratch_shapes=[vmem(p.rows, p.cols), pltpu.SemaphoreType.DMA((3,))],
+        compiler_params=pltpu.CompilerParams(vmem_limit_bytes=8 * 2**20),
+        name="outputs",
+    )(new, right, left)
 
 
 def solution(mesh):

time: 85.9 us -> 83.5 us (0.972)
  local copies, waits for them, and re-layouts: 2.74 us -> 0 us
    unnamed x4 -> x0, local copies, waits for them, and re-layouts: 2.74 us -> none
    pallas_call x1 -> x2, Pallas kernels: 82.3 us -> 82.7 us  [the longest x1 81.3 us: local_step(): pl.pallas_call(functools.partial(kernel, p), out_shape=(shaped(p.rows, p....]
where the time goes in v3:
time: 83.5 us; the launch traced here: 83.3 us
  Pallas kernels  82.7 us (99%)
    pallas_call x1, Pallas kernels, local_step(): pl.pallas_call(functools.partial(kernel, p), out_shape=(shaped(p.rows, p....  81.3 us

profile of v3, /device:TPU:1, one launch (start us, length us, event | category | flops | bytes accessed | tf_op | source)
XLA Modules:
  0.0 83.3 jit_solution(14423847224999042003)
XLA Ops:
  0.6 81.3 %dion.1 = (f32[128,1024]{1,0:T(8,128)S(1)}, f32[2,256,512]{2,1,0:T(8,128)S(1)}, f32[128,256]{1,0:T(8,128)S(1)}) custom-call(f32[128,1024]{1,0:T(8,128)} %m_hbm.1, f32[1024,256]{1,0:T(8,128)} %q_hbm.1), custom_call_target="tpu_custom_call" | custom-call | tf_op jit(solution)/shard_map/dion/pallas_call | solution.py:449
  81.9 1.4 %outputs.1 = (f32[128,1024]{1,0:T(8,128)}, f32[128,1024]{1,0:T(8,128)}) custom-call(f32[128,1024]{1,0:T(8,128)S(1)} %get-tuple-element.5.new_ref, f32[2,256,512]{2,1,0:T(8,128)S(1)} %get-tuple-element.6.right_ref, f32[128,256]{1,0:T(8,128)S(1)} %get-tuple-element.7.left_ref), custom_call_target="tpu_custom_call" | custom-call | tf_op jit(solution)/shard_map/outputs/pallas_call | solution.py:491

commit v4 on v3

--- a/solution.py
+++ b/solution.py
@@ -19,25 +19,11 @@
 HIGHEST = lax.Precision.HIGHEST
 MESH = pl.DeviceIdType.MESH
 
+A_CHUNKS = 3
 STAGES = (
-    "left_rs",
-    "left_ag",
-    "gram_core",
-    "gram_y",
-    "gram_x",
-    "gram_yag",
-    "gram_cag",
-    "w_core",
-    "wa_x",
-    "wa_y",
-    "wa_yag",
-    "wa_xag",
-    "wb_y",
-    "wb_x",
-    "wb_xag",
-    "wb_yag",
-    "right_core",
-    "norm",
+    ("left_rs", "left_ag", "gram_core", "gram_y", "gram_x", "gram_yag", "gram_cag", "w_core")
+    + tuple(f"wa{i}_{s}" for i in range(A_CHUNKS) for s in ("x", "y", "yag", "xag"))
+    + ("wb_y", "wb_x", "wb_xag", "wb_yag", "right_core", "norm")
 )
 
 
@@ -45,6 +31,21 @@
     return lax.dot_general(
         a, b, (contract, ((), ())), precision=HIGHEST, preferred_element_type=jnp.float32
     )
+
+
+def split(v):
+    high = v.astype(jnp.bfloat16)
+    return high, (v - high.astype(jnp.float32)).astype(jnp.bfloat16)
+
+
+def dot3(a, b):
+    a_high, a_low = split(a)
+    b_high, b_low = split(b)
+
+    def one(u, v):
+        return lax.dot_general(u, v, (((1,), (0,)), ((), ())), preferred_element_type=jnp.float32)
+
+    return one(a_high, b_high) + (one(a_high, b_low) + one(a_low, b_high))
 
 
 def invert_cholesky_block(work):
@@ -95,11 +96,12 @@
         self.hcols = cols // 2
         self.piece = rows // nz
         self.gpiece = self.half // ny
-        self.ax = self.half // nx
+        self.chunk = rank // (A_CHUNKS + 1)
+        self.ax = self.chunk // nx
         self.ay_rows = max(8, self.ax // ny)
         self.ay_split = ny * self.ay_rows // self.ax
         self.ay_cols = self.hcols // self.ay_split
-        self.by = self.half // ny
+        self.by = self.chunk // ny
         self.bx_rows = max(8, self.by // nx)
         self.bx_split = nx * self.bx_rows // self.by
         self.bx_cols = self.hcols // self.bx_split
@@ -236,7 +238,7 @@
     left_t[...] = left_now.T
     gram_part[...] = dot(left_t[...], left_now)
     push("gram_core", rows_of(gram_part, (1 - c) * half, half), gram_core, other)
-    w_part[...] = dot(left_t[...], m_ref[:, span((1 - c) * hcols, hcols, 128)])
+    w_part[...] = dot3(left_t[...], m_ref[:, span((1 - c) * hcols, hcols, 128)])
     push("w_core", w_part, w_core, other)
     landed("gram_core", gram_core)
     gram_half[...] = gram_part[span(c * half, half), :] + gram_core[...]
@@ -246,20 +248,103 @@
         push("gram_y", rows_of(gram_half, to * gpiece, gpiece), rows_of(gram_y, (t - 1) * gpiece, gpiece), at_y(to))
 
     each(ny, gram_y_send)
-    w_half[...] = dot(left_t[...], m_ref[:, span(c * hcols, hcols, 128)])
+    w_half[...] = dot3(left_t[...], m_ref[:, span(c * hcols, hcols, 128)])
     landed("w_core", w_core)
     w_half[...] = w_half[...] + w_core[...]
-
-    def wa_x_send(t):
-        to = (x + t) % nx
-        push("wa_x", rows_of(w_half, to * p.ax, p.ax), rows_of(wa_in, (t - 1) * p.ax, p.ax), at_x(to))
-
-    def wb_y_send(t):
-        to = (y + t) % ny
-        push("wb_y", rows_of(w_half, half + to * p.by, p.by), rows_of(wb_in, (t - 1) * p.by, p.by), at_y(to))
-
-    each(nx, wa_x_send)
-    each(ny, wb_y_send)
+    base_b = A_CHUNKS * p.chunk
+
+    def a_piece(ref, base, k):
+        return ref.at[
+            span(base + (k // p.ay_split) * p.ay_rows, p.ay_rows),
+            span((k % p.ay_split) * p.ay_cols, p.ay_cols, 128),
+        ]
+
+    def b_piece(ref, base, k):
+        return ref.at[
+            span(base + (k // p.bx_split) * p.bx_rows, p.bx_rows),
+            span((k % p.bx_split) * p.bx_cols, p.bx_cols, 128),
+        ]
+
+    def a_start(i):
+        def send_x(t):
+            to = (x + t) % nx
+            push(
+                f"wa{i}_x",
+                rows_of(w_half, i * p.chunk + to * p.ax, p.ax),
+                rows_of(wa_in.at[i], (t - 1) * p.ax, p.ax),
+                at_x(to),
+            )
+
+        each(nx, send_x)
+
+    def b_start():
+        def send_y(t):
+            to = (y + t) % ny
+            push("wb_y", rows_of(w_half, base_b + to * p.by, p.by), rows_of(wb_in, (t - 1) * p.by, p.by), at_y(to))
+
+        each(ny, send_y)
+
+    def a_second(i):
+        def send_y(t):
+            to = (y + t) % ny
+            push(
+                f"wa{i}_y",
+                a_piece(wa_sum.at[i], 0, to),
+                rows_of(wa_piece_in.at[i], (t - 1) * p.ay_rows, p.ay_rows),
+                at_y(to),
+            )
+
+        landed(f"wa{i}_x", wa_in.at[i])
+        total = w_half[span(i * p.chunk + x * p.ax, p.ax), :]
+        for t in range(nx - 1):
+            total = total + wa_in[i, t * p.ax : (t + 1) * p.ax, :]
+        wa_sum[i] = total
+        each(ny, send_y)
+
+    def b_second():
+        def send_x(t):
+            to = (x + t) % nx
+            push("wb_x", b_piece(wb_sum, 0, to), rows_of(wb_piece_in, (t - 1) * p.bx_rows, p.bx_rows), at_x(to))
+
+        landed("wb_y", wb_in)
+        total = w_half[span(base_b + y * p.by, p.by), :]
+        for t in range(ny - 1):
+            total = total + wb_in[t * p.by : (t + 1) * p.by, :]
+        wb_sum[...] = total
+        each(nx, send_x)
+
+    def a_gather(i):
+        landed(f"wa{i}_y", wa_piece_in.at[i])
+        total = a_piece(wa_sum.at[i], 0, y)[...]
+        for t in range(ny - 1):
+            total = total + wa_piece_in[i, t * p.ay_rows : (t + 1) * p.ay_rows, :]
+        mine_w = a_piece(w_full, i * p.chunk + x * p.ax, y)
+        mine_w[...] = total
+        each(ny, lambda t: push(f"wa{i}_yag", mine_w, mine_w, at_y((y + t) % ny)))
+
+    def b_gather():
+        landed("wb_x", wb_piece_in)
+        total = b_piece(wb_sum, 0, x)[...]
+        for t in range(nx - 1):
+            total = total + wb_piece_in[t * p.bx_rows : (t + 1) * p.bx_rows, :]
+        mine_b = b_piece(w_full, base_b + y * p.by, x)
+        mine_b[...] = total
+        each(nx, lambda t: push("wb_xag", mine_b, mine_b, at_x((x + t) % nx)))
+
+    def a_last(i):
+        landed(f"wa{i}_yag", wa_piece_in.at[i])
+        rows_a = rows_of(w_full, i * p.chunk + x * p.ax, p.ax)
+        each(nx, lambda t: push(f"wa{i}_xag", rows_a, rows_a, at_x((x + t) % nx)))
+
+    def b_last():
+        landed("wb_xag", wb_piece_in)
+        rows_b = rows_of(w_full, base_b + y * p.by, p.by)
+        each(ny, lambda t: push("wb_yag", rows_b, rows_b, at_y((y + t) % ny)))
+
+    for i in range(A_CHUNKS):
+        a_start(i)
+    b_start()
+    a_second(0)
     landed("gram_y", gram_y)
     total = gram_half[span(y * gpiece, gpiece), :]
     for t in range(ny - 1):
@@ -267,6 +352,9 @@
     gram_x[span(x * gpiece, gpiece), :] = total
     mine_g = rows_of(gram_x, x * gpiece, gpiece)
     each(nx, lambda t: push("gram_x", mine_g, mine_g, at_x((x + t) % nx)))
+    for i in range(1, A_CHUNKS):
+        a_second(i)
+    b_second()
     landed("gram_x", gram_x.at[pl.ds(0, (nx - 1) * gpiece)])
     total = gram_x[0:gpiece, :]
     for t in range(1, nx):
@@ -275,61 +363,15 @@
     gram[span(at, gpiece), :] = total
     mine_a = rows_of(gram, at, gpiece)
     each(ny, lambda t: push("gram_yag", mine_a, mine_a, at_y((y + t) % ny)))
-
-    def a_piece(ref, base, k):
-        return ref.at[
-            span(base + (k // p.ay_split) * p.ay_rows, p.ay_rows),
-            span((k % p.ay_split) * p.ay_cols, p.ay_cols, 128),
-        ]
-
-    def b_piece(ref, base, k):
-        return ref.at[
-            span(base + (k // p.bx_split) * p.bx_rows, p.bx_rows),
-            span((k % p.bx_split) * p.bx_cols, p.bx_cols, 128),
-        ]
-
-    def wa_y_send(t):
-        to = (y + t) % ny
-        push("wa_y", a_piece(wa_sum, 0, to), rows_of(wa_piece_in, (t - 1) * p.ay_rows, p.ay_rows), at_y(to))
-
-    landed("wa_x", wa_in)
-    total = w_half[span(x * p.ax, p.ax), :]
-    for t in range(nx - 1):
-        total = total + wa_in[t * p.ax : (t + 1) * p.ax, :]
-    wa_sum[...] = total
-    each(ny, wa_y_send)
-
-    def wb_x_send(t):
-        to = (x + t) % nx
-        push("wb_x", b_piece(wb_sum, 0, to), rows_of(wb_piece_in, (t - 1) * p.bx_rows, p.bx_rows), at_x(to))
-
-    landed("wb_y", wb_in)
-    total = w_half[span(half + y * p.by, p.by), :]
-    for t in range(ny - 1):
-        total = total + wb_in[t * p.by : (t + 1) * p.by, :]
-    wb_sum[...] = total
-    each(nx, wb_x_send)
-
+    a_gather(0)
+    b_gather()
+    for i in range(1, A_CHUNKS):
+        a_gather(i)
+    b_last()
     landed("gram_yag", gram_y)
     mine_h = rows_of(gram, c * half, half)
     push("gram_cag", mine_h, mine_h, other)
-
-    base_a = x * p.ax
-    base_b = half + y * p.by
-    landed("wb_x", wb_piece_in)
-    total = b_piece(wb_sum, 0, x)[...]
-    for t in range(nx - 1):
-        total = total + wb_piece_in[t * p.bx_rows : (t + 1) * p.bx_rows, :]
-    mine_b = b_piece(w_full, base_b, x)
-    mine_b[...] = total
-    each(nx, lambda t: push("wb_xag", mine_b, mine_b, at_x((x + t) % nx)))
-    landed("wa_y", wa_piece_in)
-    total = a_piece(wa_sum, 0, y)[...]
-    for t in range(ny - 1):
-        total = total + wa_piece_in[t * p.ay_rows : (t + 1) * p.ay_rows, :]
-    mine_w = a_piece(w_full, base_a, y)
-    mine_w[...] = total
-    each(ny, lambda t: push("wa_yag", mine_w, mine_w, at_y((y + t) % ny)))
+    a_last(0)
     landed("gram_cag", gram_half)
 
     nb = rank // BLOCK
@@ -340,13 +382,8 @@
 
     def after_block(k):
         if k == 0:
-            landed("wb_xag", wb_piece_in)
-            rows_b = rows_of(w_full, base_b, p.by)
-            each(ny, lambda t: push("wb_yag", rows_b, rows_b, at_y((y + t) % ny)))
-        if k == 1:
-            landed("wa_yag", wa_piece_in)
-            rows_a = rows_of(w_full, base_a, p.ax)
-            each(nx, lambda t: push("wa_xag", rows_a, rows_a, at_x((x + t) % nx)))
+            for i in range(1, A_CHUNKS):
+                a_last(i)
 
     inverse_rows = []
     solved = []
@@ -373,10 +410,10 @@
             inv_row = jnp.concatenate([inv_row, jnp.zeros((BLOCK, rank - hi), jnp.float32)], axis=1)
         inverse_ref[lo:hi, :] = inv_row
         after_block(k)
-    left_orth = dot(left[...], inverse_ref[...], ((1,), (1,)))
-    landed("wa_xag", wa_in)
     landed("wb_yag", wb_in)
-    r = dot(inverse_ref[...], w_full[...])
+    for i in range(A_CHUNKS):
+        landed(f"wa{i}_xag", wa_in.at[i])
+    r = dot3(inverse_ref[...], w_full[...])
     right[c] = r
     push("right_core", right.at[c], right.at[c], other)
     folded = r[:, 0:128] * r[:, 0:128]
@@ -392,12 +429,13 @@
 
     each(nz, norm_send)
     push("norm", norm_out, norm_in.at[nz - 1], other)
+    left_orth = dot(left[...], inverse_ref[...], ((1,), (1,)))
     half_orth = 0.5 * left_orth
     mine_cols = span(c * hcols, hcols, 128)
-    new_out[:, mine_cols] = m_ref[:, mine_cols] - dot(half_orth, right[c])
+    new_out[:, mine_cols] = m_ref[:, mine_cols] - dot3(half_orth, right[c])
     landed("right_core", w_half)
     other_cols = span((1 - c) * hcols, hcols, 128)
-    new_out[:, other_cols] = m_ref[:, other_cols] - dot(half_orth, right[1 - c])
+    new_out[:, other_cols] = m_ref[:, other_cols] - dot3(half_orth, right[1 - c])
     right_out[...] = right[...]
     landed("norm", norm_in)
     total = norm_out[...]
@@ -414,10 +452,11 @@
     sent("gram_yag", gram_y)
     sent("gram_cag", gram_half)
     sent("w_core", w_core)
-    sent("wa_x", wa_in)
-    sent("wa_y", wa_piece_in)
-    sent("wa_yag", wa_piece_in)
-    sent("wa_xag", wa_in)
+    for i in range(A_CHUNKS):
+        sent(f"wa{i}_x", wa_in.at[i])
+        sent(f"wa{i}_y", wa_piece_in.at[i])
+        sent(f"wa{i}_yag", wa_piece_in.at[i])
+        sent(f"wa{i}_xag", wa_in.at[i])
     sent("wb_y", wb_in)
     sent("wb_x", wb_piece_in)
     sent("wb_xag", wb_piece_in)
@@ -432,7 +471,7 @@
     copies[0].start()
     for h in range(2):
         at = pl.ds(h * hcols, hcols)
-        upd[:, at] = dot(left_ref[...], right_ref[h])
+        upd[:, at] = dot3(left_ref[...], right_ref[h])
         copies.append(pltpu.make_async_copy(upd.at[:, at], upd_hbm.at[:, at], sems.at[1 + h]))
         copies[-1].start()
     for copy in copies:
@@ -467,10 +506,10 @@
             vmem(p.rank, p.hcols),
             vmem(p.rank, p.hcols),
             vmem(p.rank, p.hcols),
-            vmem(p.half - p.ax, p.hcols),
-            vmem(p.ax, p.hcols),
-            vmem((p.ny - 1) * p.ay_rows, p.ay_cols),
-            vmem(p.half - p.by, p.hcols),
+            vmem(A_CHUNKS, p.chunk - p.ax, p.hcols),
+            vmem(A_CHUNKS, p.ax, p.hcols),
+            vmem(A_CHUNKS, (p.ny - 1) * p.ay_rows, p.ay_cols),
+            vmem(p.chunk - p.by, p.hcols),
             vmem(p.by, p.hcols),
             vmem((p.nx - 1) * p.bx_rows, p.bx_cols),
             vmem(p.rank, p.hcols),

time: 83.5 us -> 78.4 us (0.939)
  Pallas kernels: 82.7 us -> 77.6 us
    pallas_call x1, Pallas kernels: 81.3 us -> 76.4 us  [local_step(): pl.pallas_call(functools.partial(kernel, p), out_shape=(shaped(p.rows, p....]
where the time goes in v4:
time: 78.4 us; the launch traced here: 78.2 us
  Pallas kernels  77.6 us (99%)
    pallas_call x1, Pallas kernels, local_step(): pl.pallas_call(functools.partial(kernel, p), out_shape=(shaped(p.rows, p....  76.4 us

profile of v4, /device:TPU:1, one launch (start us, length us, event | category | flops | bytes accessed | tf_op | source)
XLA Modules:
  0.0 78.2 jit_solution(961508317189599891)
XLA Ops:
  0.6 76.4 %dion.1 = (f32[128,1024]{1,0:T(8,128)S(1)}, f32[2,256,512]{2,1,0:T(8,128)S(1)}, f32[128,256]{1,0:T(8,128)S(1)}) custom-call(f32[128,1024]{1,0:T(8,128)} %m_hbm.1, f32[1024,256]{1,0:T(8,128)} %q_hbm.1), custom_call_target="tpu_custom_call" | custom-call | tf_op jit(solution)/shard_map/dion/pallas_call | solution.py:488
  77.0 1.2 %outputs.1 = (f32[128,1024]{1,0:T(8,128)}, f32[128,1024]{1,0:T(8,128)}) custom-call(f32[128,1024]{1,0:T(8,128)S(1)} %get-tuple-element.5.new_ref, f32[2,256,512]{2,1,0:T(8,128)S(1)} %get-tuple-element.6.right_ref, f32[128,256]{1,0:T(8,128)S(1)} %get-tuple-element.7.left_ref), custom_call_target="tpu_custom_call" | custom-call | tf_op jit(solution)/shard_map/outputs/pallas_call | solution.py:530

commit v5 on v4

--- a/solution.py
+++ b/solution.py
@@ -21,7 +21,7 @@
 
 A_CHUNKS = 3
 STAGES = (
-    ("left_rs", "left_ag", "gram_core", "gram_y", "gram_x", "gram_yag", "gram_cag", "w_core")
+    ("left_rs", "left_ag", "m_core", "left_core", "gram_y", "gram_x", "gram_yag", "gram_cag")
     + tuple(f"wa{i}_{s}" for i in range(A_CHUNKS) for s in ("x", "y", "yag", "xag"))
     + ("wb_y", "wb_x", "wb_xag", "wb_yag", "right_core", "norm")
 )
@@ -95,7 +95,8 @@
         self.half = rank // 2
         self.hcols = cols // 2
         self.piece = rows // nz
-        self.gpiece = self.half // ny
+        self.ghalf = 3 * self.half // 2
+        self.gpiece = self.ghalf // ny
         self.chunk = rank // (A_CHUNKS + 1)
         self.ax = self.chunk // nx
         self.ay_rows = max(8, self.ax // ny)
@@ -119,15 +120,13 @@
     part,
     left_in,
     left,
+    left_other,
+    m_other,
     gram_part,
-    gram_core,
-    gram_half,
     gram_y,
     gram_x,
     gram,
     work,
-    w_part,
-    w_core,
     w_half,
     wa_in,
     wa_sum,
@@ -145,7 +144,7 @@
     local,
 ):
     nx, ny, nz, rank = p.nx, p.ny, p.nz, p.rank
-    half, hcols, piece, gpiece = p.half, p.hcols, p.piece, p.gpiece
+    half, hcols, piece, ghalf, gpiece = p.half, p.hcols, p.piece, p.ghalf, p.gpiece
     row_at = lax.axis_index("row")
     z = lax.axis_index("col")
     c = row_at % CORES
@@ -205,14 +204,17 @@
     def greet(target):
         pl.semaphore_signal(barrier, inc=1, device_id=target, device_id_type=MESH)
 
-    each(nz, lambda t: greet(at_z((z + t) % nz)))
+    def greet_z(t):
+        greet(at_z((z + t) % nz))
+        greet(at_z_other((z + t) % nz))
+
+    each(nz, greet_z)
     load_m = pltpu.make_async_copy(m_hbm, m_ref, local.at[0])
     load_q = pltpu.make_async_copy(q_hbm, q_ref, local.at[1])
     load_m.start()
     load_q.start()
     each(ny, lambda t: greet(at_y((y + t) % ny)))
     each(nx, lambda t: greet(at_x((x + t) % nx)))
-    each(nz, lambda t: greet(at_z_other((z + t) % nz)))
     greet(other)
     load_m.wait()
     load_q.wait()
@@ -224,6 +226,9 @@
         push("left_rs", rows_of(part, to * piece, piece), rows_of(left_in, (t - 1) * piece, piece), at_z(to))
 
     each(nz, left_send)
+    mine_cols = span(c * hcols, hcols, 128)
+    other_cols = span((1 - c) * hcols, hcols, 128)
+    push("m_core", m_ref.at[:, other_cols], m_other, other)
     landed("left_rs", left_in)
     total = part[span(z * piece, piece), :]
     for t in range(nz - 1):
@@ -233,24 +238,31 @@
     each(nz, lambda t: push("left_ag", mine, mine, at_z((z + t) % nz)))
     landed("left_ag", left_in)
 
+    push("left_core", left, left_other, other)
     left_now = left[...]
-    left_t = work.at[:, 0 : p.rows]
-    left_t[...] = left_now.T
-    gram_part[...] = dot(left_t[...], left_now)
-    push("gram_core", rows_of(gram_part, (1 - c) * half, half), gram_core, other)
-    w_part[...] = dot3(left_t[...], m_ref[:, span((1 - c) * hcols, hcols, 128)])
-    push("w_core", w_part, w_core, other)
-    landed("gram_core", gram_core)
-    gram_half[...] = gram_part[span(c * half, half), :] + gram_core[...]
+    left_t = left_now.T
+    gram_own = dot(left_t, left_now)
+    w_half[...] = dot3(left_t, m_ref[:, mine_cols])
+    landed("left_core", left_other)
+    left_now = left_other[...]
+    left_t = left_now.T
+    gram_pair = gram_own + dot(left_t, left_now)
+    gram_part[0:half, :] = gram_pair[0:half, 0:half]
+    gram_part[half : 2 * half, :] = gram_pair[0:half, half:]
+    gram_part[2 * half :, :] = gram_pair[half:, half:]
 
     def gram_y_send(t):
         to = (y + t) % ny
-        push("gram_y", rows_of(gram_half, to * gpiece, gpiece), rows_of(gram_y, (t - 1) * gpiece, gpiece), at_y(to))
+        push(
+            "gram_y",
+            rows_of(gram_part, c * ghalf + to * gpiece, gpiece),
+            rows_of(gram_y, (t - 1) * gpiece, gpiece),
+            at_y(to),
+        )
 
     each(ny, gram_y_send)
-    w_half[...] = dot3(left_t[...], m_ref[:, span(c * hcols, hcols, 128)])
-    landed("w_core", w_core)
-    w_half[...] = w_half[...] + w_core[...]
+    landed("m_core", m_other)
+    w_half[...] = w_half[...] + dot3(left_t, m_other[...])
     base_b = A_CHUNKS * p.chunk
 
     def a_piece(ref, base, k):
@@ -346,7 +358,7 @@
     b_start()
     a_second(0)
     landed("gram_y", gram_y)
-    total = gram_half[span(y * gpiece, gpiece), :]
+    total = gram_part[span(c * ghalf + y * gpiece, gpiece), :]
     for t in range(ny - 1):
         total = total + gram_y[t * gpiece : (t + 1) * gpiece, :]
     gram_x[span(x * gpiece, gpiece), :] = total
@@ -359,7 +371,7 @@
     total = gram_x[0:gpiece, :]
     for t in range(1, nx):
         total = total + gram_x[t * gpiece : (t + 1) * gpiece, :]
-    at = c * half + y * gpiece
+    at = c * ghalf + y * gpiece
     gram[span(at, gpiece), :] = total
     mine_a = rows_of(gram, at, gpiece)
     each(ny, lambda t: push("gram_yag", mine_a, mine_a, at_y((y + t) % ny)))
@@ -367,23 +379,25 @@
     b_gather()
     for i in range(1, A_CHUNKS):
         a_gather(i)
+    landed("gram_yag", gram_y)
+    mine_h = rows_of(gram, c * ghalf, ghalf)
+    push("gram_cag", mine_h, mine_h, other)
     b_last()
-    landed("gram_yag", gram_y)
-    mine_h = rows_of(gram, c * half, half)
-    push("gram_cag", mine_h, mine_h, other)
     a_last(0)
-    landed("gram_cag", gram_half)
+    landed("gram_cag", mine_h)
 
     nb = rank // BLOCK
-    work[...] = gram[...]
+    work[0:half, 0:half] = gram[0:half, :]
+    work[0:half, half:] = gram[half : 2 * half, :]
+    work[half:, 0:half] = jnp.zeros((half, half), jnp.float32)
+    work[half:, half:] = gram[2 * half :, :]
     eye = (
         lax.broadcasted_iota(jnp.int32, (BLOCK, BLOCK), 0) == lax.broadcasted_iota(jnp.int32, (BLOCK, BLOCK), 1)
     ).astype(jnp.float32)
 
     def after_block(k):
-        if k == 0:
-            for i in range(1, A_CHUNKS):
-                a_last(i)
+        if k + 1 < A_CHUNKS:
+            a_last(k + 1)
 
     inverse_rows = []
     solved = []
@@ -431,10 +445,8 @@
     push("norm", norm_out, norm_in.at[nz - 1], other)
     left_orth = dot(left[...], inverse_ref[...], ((1,), (1,)))
     half_orth = 0.5 * left_orth
-    mine_cols = span(c * hcols, hcols, 128)
     new_out[:, mine_cols] = m_ref[:, mine_cols] - dot3(half_orth, right[c])
     landed("right_core", w_half)
-    other_cols = span((1 - c) * hcols, hcols, 128)
     new_out[:, other_cols] = m_ref[:, other_cols] - dot3(half_orth, right[1 - c])
     right_out[...] = right[...]
     landed("norm", norm_in)
@@ -446,12 +458,12 @@
 
     sent("left_rs", left_in)
     sent("left_ag", left_in)
-    sent("gram_core", gram_core)
+    sent("m_core", m_other)
+    sent("left_core", left_other)
     sent("gram_y", gram_y)
     sent("gram_x", gram_x.at[pl.ds(0, (nx - 1) * gpiece)])
     sent("gram_yag", gram_y)
-    sent("gram_cag", gram_half)
-    sent("w_core", w_core)
+    sent("gram_cag", mine_h)
     for i in range(A_CHUNKS):
         sent(f"wa{i}_x", wa_in.at[i])
         sent(f"wa{i}_y", wa_piece_in.at[i])
@@ -496,15 +508,13 @@
             vmem(p.rows, p.rank),
             vmem(p.rows - p.piece, p.rank),
             vmem(p.rows, p.rank),
+            vmem(p.rows, p.rank),
+            vmem(p.rows, p.hcols),
+            vmem(2 * p.ghalf, p.half),
+            vmem(p.ghalf - p.gpiece, p.half),
+            vmem(p.nx * p.gpiece, p.half),
+            vmem(2 * p.ghalf, p.half),
             vmem(p.rank, p.rank),
-            vmem(p.half, p.rank),
-            vmem(p.half, p.rank),
-            vmem(p.half - p.gpiece, p.rank),
-            vmem(p.nx * p.gpiece, p.rank),
-            vmem(p.rank, p.rank),
-            vmem(p.rank, p.rank),
-            vmem(p.rank, p.hcols),
-            vmem(p.rank, p.hcols),
             vmem(p.rank, p.hcols),
             vmem(A_CHUNKS, p.chunk - p.ax, p.hcols),
             vmem(A_CHUNKS, p.ax, p.hcols),

time: 78.4 us -> 76.7 us (0.978)
  Pallas kernels: 77.6 us -> 75.9 us
    pallas_call x1, Pallas kernels: 76.4 us -> 74.8 us  [local_step(): pl.pallas_call(functools.partial(kernel, p), out_shape=(shaped(p.rows, p....]
where the time goes in v5:
time: 76.7 us; the launch traced here: 76.6 us
  Pallas kernels  75.9 us (99%)
    pallas_call x1, Pallas kernels, local_step(): pl.pallas_call(functools.partial(kernel, p), out_shape=(shaped(p.rows, p....  74.8 us

profile of v5, /device:TPU:1, one launch (start us, length us, event | category | flops | bytes accessed | tf_op | source)
XLA Modules:
  0.0 76.6 jit_solution(2065580999547956138)
XLA Ops:
  0.6 74.8 %dion.1 = (f32[128,1024]{1,0:T(8,128)S(1)}, f32[2,256,512]{2,1,0:T(8,128)S(1)}, f32[128,256]{1,0:T(8,128)S(1)}) custom-call(f32[128,1024]{1,0:T(8,128)} %m_hbm.1, f32[1024,256]{1,0:T(8,128)} %q_hbm.1), custom_call_target="tpu_custom_call" | custom-call | tf_op jit(solution)/shard_map/dion/pallas_call | solution.py:500
  75.4 1.2 %outputs.1 = (f32[128,1024]{1,0:T(8,128)}, f32[128,1024]{1,0:T(8,128)}) custom-call(f32[128,1024]{1,0:T(8,128)S(1)} %get-tuple-element.5.new_ref, f32[2,256,512]{2,1,0:T(8,128)S(1)} %get-tuple-element.6.right_ref, f32[128,256]{1,0:T(8,128)S(1)} %get-tuple-element.7.left_ref), custom_call_target="tpu_custom_call" | custom-call | tf_op jit(solution)/shard_map/outputs/pallas_call | solution.py:540

commit v6 on v5

--- a/solution.py
+++ b/solution.py
@@ -147,9 +147,9 @@
     half, hcols, piece, ghalf, gpiece = p.half, p.hcols, p.piece, p.ghalf, p.gpiece
     row_at = lax.axis_index("row")
     z = lax.axis_index("col")
-    c = row_at % CORES
-    y = (row_at // CORES) % ny
-    x = row_at // (CORES * ny)
+    c = lax.rem(row_at, CORES)
+    y = lax.rem(lax.div(row_at, CORES), ny)
+    x = lax.div(row_at, CORES * ny)
     other_row = (x * ny + y) * CORES + (1 - c)
     other = {"row": other_row}
 
@@ -188,16 +188,9 @@
     def rows_of(ref, start, size):
         return ref.at[span(start, size)]
 
-    def far_first(t, n):
-        h = t // 2
-        return n // 2 + h * (2 * (t % 2) - 1)
-
     def each(n, fn):
-        def body(t, carry):
-            fn(far_first(t, n))
-            return carry
-
-        lax.fori_loop(1, n, body, 0)
+        for t in sorted(range(1, n), key=lambda t: -min(t, n - t)):
+            fn(t)
 
     barrier = pltpu.get_barrier_semaphore()
 
@@ -205,16 +198,16 @@
         pl.semaphore_signal(barrier, inc=1, device_id=target, device_id_type=MESH)
 
     def greet_z(t):
-        greet(at_z((z + t) % nz))
-        greet(at_z_other((z + t) % nz))
+        greet(at_z(lax.rem(z + t, nz)))
+        greet(at_z_other(lax.rem(z + t, nz)))
 
     each(nz, greet_z)
     load_m = pltpu.make_async_copy(m_hbm, m_ref, local.at[0])
     load_q = pltpu.make_async_copy(q_hbm, q_ref, local.at[1])
     load_m.start()
     load_q.start()
-    each(ny, lambda t: greet(at_y((y + t) % ny)))
-    each(nx, lambda t: greet(at_x((x + t) % nx)))
+    each(ny, lambda t: greet(at_y(lax.rem(y + t, ny))))
+    each(nx, lambda t: greet(at_x(lax.rem(x + t, nx))))
     greet(other)
     load_m.wait()
     load_q.wait()
@@ -222,7 +215,7 @@
     pl.semaphore_wait(barrier, 2 * nz + ny + nx - 3)
 
     def left_send(t):
-        to = (z + t) % nz
+        to = lax.rem(z + t, nz)
         push("left_rs", rows_of(part, to * piece, piece), rows_of(left_in, (t - 1) * piece, piece), at_z(to))
 
     each(nz, left_send)
@@ -235,7 +228,7 @@
         total = total + left_in[t * piece : (t + 1) * piece, :]
     left[span(z * piece, piece), :] = total
     mine = rows_of(left, z * piece, piece)
-    each(nz, lambda t: push("left_ag", mine, mine, at_z((z + t) % nz)))
+    each(nz, lambda t: push("left_ag", mine, mine, at_z(lax.rem(z + t, nz))))
     landed("left_ag", left_in)
 
     push("left_core", left, left_other, other)
@@ -252,7 +245,7 @@
     gram_part[2 * half :, :] = gram_pair[half:, half:]
 
     def gram_y_send(t):
-        to = (y + t) % ny
+        to = lax.rem(y + t, ny)
         push(
             "gram_y",
             rows_of(gram_part, c * ghalf + to * gpiece, gpiece),
@@ -267,19 +260,19 @@
 
     def a_piece(ref, base, k):
         return ref.at[
-            span(base + (k // p.ay_split) * p.ay_rows, p.ay_rows),
-            span((k % p.ay_split) * p.ay_cols, p.ay_cols, 128),
+            span(base + lax.div(k, p.ay_split) * p.ay_rows, p.ay_rows),
+            span(lax.rem(k, p.ay_split) * p.ay_cols, p.ay_cols, 128),
         ]
 
     def b_piece(ref, base, k):
         return ref.at[
-            span(base + (k // p.bx_split) * p.bx_rows, p.bx_rows),
-            span((k % p.bx_split) * p.bx_cols, p.bx_cols, 128),
+            span(base + lax.div(k, p.bx_split) * p.bx_rows, p.bx_rows),
+            span(lax.rem(k, p.bx_split) * p.bx_cols, p.bx_cols, 128),
         ]
 
     def a_start(i):
         def send_x(t):
-            to = (x + t) % nx
+            to = lax.rem(x + t, nx)
             push(
                 f"wa{i}_x",
                 rows_of(w_half, i * p.chunk + to * p.ax, p.ax),
@@ -291,14 +284,14 @@
 
     def b_start():
         def send_y(t):
-            to = (y + t) % ny
+            to = lax.rem(y + t, ny)
             push("wb_y", rows_of(w_half, base_b + to * p.by, p.by), rows_of(wb_in, (t - 1) * p.by, p.by), at_y(to))
 
         each(ny, send_y)
 
     def a_second(i):
         def send_y(t):
-            to = (y + t) % ny
+            to = lax.rem(y + t, ny)
             push(
                 f"wa{i}_y",
                 a_piece(wa_sum.at[i], 0, to),
@@ -315,7 +308,7 @@
 
     def b_second():
         def send_x(t):
-            to = (x + t) % nx
+            to = lax.rem(x + t, nx)
             push("wb_x", b_piece(wb_sum, 0, to), rows_of(wb_piece_in, (t - 1) * p.bx_rows, p.bx_rows), at_x(to))
 
         landed("wb_y", wb_in)
@@ -332,7 +325,7 @@
             total = total + wa_piece_in[i, t * p.ay_rows : (t + 1) * p.ay_rows, :]
         mine_w = a_piece(w_full, i * p.chunk + x * p.ax, y)
         mine_w[...] = total
-        each(ny, lambda t: push(f"wa{i}_yag", mine_w, mine_w, at_y((y + t) % ny)))
+        each(ny, lambda t: push(f"wa{i}_yag", mine_w, mine_w, at_y(lax.rem(y + t, ny))))
 
     def b_gather():
         landed("wb_x", wb_piece_in)
@@ -341,17 +334,17 @@
             total = total + wb_piece_in[t * p.bx_rows : (t + 1) * p.bx_rows, :]
         mine_b = b_piece(w_full, base_b + y * p.by, x)
         mine_b[...] = total
-        each(nx, lambda t: push("wb_xag", mine_b, mine_b, at_x((x + t) % nx)))
+        each(nx, lambda t: push("wb_xag", mine_b, mine_b, at_x(lax.rem(x + t, nx))))
 
     def a_last(i):
         landed(f"wa{i}_yag", wa_piece_in.at[i])
         rows_a = rows_of(w_full, i * p.chunk + x * p.ax, p.ax)
-        each(nx, lambda t: push(f"wa{i}_xag", rows_a, rows_a, at_x((x + t) % nx)))
+        each(nx, lambda t: push(f"wa{i}_xag", rows_a, rows_a, at_x(lax.rem(x + t, nx))))
 
     def b_last():
         landed("wb_xag", wb_piece_in)
         rows_b = rows_of(w_full, base_b + y * p.by, p.by)
-        each(ny, lambda t: push("wb_yag", rows_b, rows_b, at_y((y + t) % ny)))
+        each(ny, lambda t: push("wb_yag", rows_b, rows_b, at_y(lax.rem(y + t, ny))))
 
     for i in range(A_CHUNKS):
         a_start(i)
@@ -363,7 +356,7 @@
         total = total + gram_y[t * gpiece : (t + 1) * gpiece, :]
     gram_x[span(x * gpiece, gpiece), :] = total
     mine_g = rows_of(gram_x, x * gpiece, gpiece)
-    each(nx, lambda t: push("gram_x", mine_g, mine_g, at_x((x + t) % nx)))
+    each(nx, lambda t: push("gram_x", mine_g, mine_g, at_x(lax.rem(x + t, nx))))
     for i in range(1, A_CHUNKS):
         a_second(i)
     b_second()
@@ -374,7 +367,7 @@
     at = c * ghalf + y * gpiece
     gram[span(at, gpiece), :] = total
     mine_a = rows_of(gram, at, gpiece)
-    each(ny, lambda t: push("gram_yag", mine_a, mine_a, at_y((y + t) % ny)))
+    each(ny, lambda t: push("gram_yag", mine_a, mine_a, at_y(lax.rem(y + t, ny))))
     a_gather(0)
     b_gather()
     for i in range(1, A_CHUNKS):
@@ -437,7 +430,7 @@
     norm_out[...] = squares[0:1, :]
 
     def norm_send(t):
-        to = (z + t) % nz
+        to = lax.rem(z + t, nz)
         push("norm", norm_out, norm_in.at[t - 1], at_z(to))
         push("norm", norm_out, norm_in.at[nz - 1 + t], at_z_other(to))
 

time: 76.7 us -> 77 us (level)
  no operation moved by 1% of the time
where the time goes in v6:
time: 77 us; the launch traced here: 76.8 us
  Pallas kernels  76.2 us (99%)
    pallas_call x1, Pallas kernels, local_step(): pl.pallas_call(functools.partial(kernel, p), out_shape=(shaped(p.rows, p....  75 us

profile of v6, /device:TPU:1, one launch (start us, length us, event | category | flops | bytes accessed | tf_op | source)
XLA Modules:
  0.0 76.8 jit_solution(15933285701415318586)
XLA Ops:
  0.6 75.0 %dion.1 = (f32[128,1024]{1,0:T(8,128)S(1)}, f32[2,256,512]{2,1,0:T(8,128)S(1)}, f32[128,256]{1,0:T(8,128)S(1)}) custom-call(f32[128,1024]{1,0:T(8,128)} %m_hbm.1, f32[1024,256]{1,0:T(8,128)} %q_hbm.1), custom_call_target="tpu_custom_call" | custom-call | tf_op jit(solution)/shard_map/dion/pallas_call | solution.py:493
  75.6 1.2 %outputs.1 = (f32[128,1024]{1,0:T(8,128)}, f32[128,1024]{1,0:T(8,128)}) custom-call(f32[128,1024]{1,0:T(8,128)S(1)} %get-tuple-element.5.new_ref, f32[2,256,512]{2,1,0:T(8,128)S(1)} %get-tuple-element.6.right_ref, f32[128,256]{1,0:T(8,128)S(1)} %get-tuple-element.7.left_ref), custom_call_target="tpu_custom_call" | custom-call | tf_op jit(solution)/shard_map/outputs/pallas_call | solution.py:533

commit v7 on v6

--- a/solution.py
+++ b/solution.py
@@ -234,26 +234,11 @@
     push("left_core", left, left_other, other)
     left_now = left[...]
     left_t = left_now.T
+    w_half[...] = dot3(left_t, m_ref[:, mine_cols])
     gram_own = dot(left_t, left_now)
-    w_half[...] = dot3(left_t, m_ref[:, mine_cols])
     landed("left_core", left_other)
     left_now = left_other[...]
     left_t = left_now.T
-    gram_pair = gram_own + dot(left_t, left_now)
-    gram_part[0:half, :] = gram_pair[0:half, 0:half]
-    gram_part[half : 2 * half, :] = gram_pair[0:half, half:]
-    gram_part[2 * half :, :] = gram_pair[half:, half:]
-
-    def gram_y_send(t):
-        to = lax.rem(y + t, ny)
-        push(
-            "gram_y",
-            rows_of(gram_part, c * ghalf + to * gpiece, gpiece),
-            rows_of(gram_y, (t - 1) * gpiece, gpiece),
-            at_y(to),
-        )
-
-    each(ny, gram_y_send)
     landed("m_core", m_other)
     w_half[...] = w_half[...] + dot3(left_t, m_other[...])
     base_b = A_CHUNKS * p.chunk
@@ -348,6 +333,21 @@
 
     for i in range(A_CHUNKS):
         a_start(i)
+    gram_pair = gram_own + dot(left_t, left_now)
+    gram_part[0:half, :] = gram_pair[0:half, 0:half]
+    gram_part[half : 2 * half, :] = gram_pair[0:half, half:]
+    gram_part[2 * half :, :] = gram_pair[half:, half:]
+
+    def gram_y_send(t):
+        to = lax.rem(y + t, ny)
+        push(
+            "gram_y",
+            rows_of(gram_part, c * ghalf + to * gpiece, gpiece),
+            rows_of(gram_y, (t - 1) * gpiece, gpiece),
+            at_y(to),
+        )
+
+    each(ny, gram_y_send)
     b_start()
     a_second(0)
     landed("gram_y", gram_y)
@@ -417,10 +417,14 @@
             inv_row = jnp.concatenate([inv_row, jnp.zeros((BLOCK, rank - hi), jnp.float32)], axis=1)
         inverse_ref[lo:hi, :] = inv_row
         after_block(k)
+    for i in range(2):
+        landed(f"wa{i}_xag", wa_in.at[i])
+    first = 2 * p.chunk
+    r = dot3(inverse_ref[:, 0:first], w_full[0:first, :])
     landed("wb_yag", wb_in)
-    for i in range(A_CHUNKS):
+    for i in range(2, A_CHUNKS):
         landed(f"wa{i}_xag", wa_in.at[i])
-    r = dot3(inverse_ref[...], w_full[...])
+    r = r + dot3(inverse_ref[:, first:], w_full[first:, :])
     right[c] = r
     push("right_core", right.at[c], right.at[c], other)
     folded = r[:, 0:128] * r[:, 0:128]

time: 77 us -> 77.2 us (level)
  no operation moved by 1% of the time
where the time goes in v7:
time: 77.2 us; the launch traced here: 77 us
  Pallas kernels  76.4 us (99%)
    pallas_call x1, Pallas kernels, local_step(): pl.pallas_call(functools.partial(kernel, p), out_shape=(shaped(p.rows, p....  75.2 us

profile of v7, /device:TPU:1, one launch (start us, length us, event | category | flops | bytes accessed | tf_op | source)
XLA Modules:
  0.0 77.0 jit_solution(12548351932259671979)
XLA Ops:
  0.6 75.2 %dion.1 = (f32[128,1024]{1,0:T(8,128)S(1)}, f32[2,256,512]{2,1,0:T(8,128)S(1)}, f32[128,256]{1,0:T(8,128)S(1)}) custom-call(f32[128,1024]{1,0:T(8,128)} %m_hbm.1, f32[1024,256]{1,0:T(8,128)} %q_hbm.1), custom_call_target="tpu_custom_call" | custom-call | tf_op jit(solution)/shard_map/dion/pallas_call | solution.py:497
  75.9 1.2 %outputs.1 = (f32[128,1024]{1,0:T(8,128)}, f32[128,1024]{1,0:T(8,128)}) custom-call(f32[128,1024]{1,0:T(8,128)S(1)} %get-tuple-element.5.new_ref, f32[2,256,512]{2,1,0:T(8,128)S(1)} %get-tuple-element.6.right_ref, f32[128,256]{1,0:T(8,128)S(1)} %get-tuple-element.7.left_ref), custom_call_target="tpu_custom_call" | custom-call | tf_op jit(solution)/shard_map/outputs/pallas_call | solution.py:537

commit v8 on v6

--- a/solution.py
+++ b/solution.py
@@ -417,10 +417,14 @@
             inv_row = jnp.concatenate([inv_row, jnp.zeros((BLOCK, rank - hi), jnp.float32)], axis=1)
         inverse_ref[lo:hi, :] = inv_row
         after_block(k)
+    for i in range(2):
+        landed(f"wa{i}_xag", wa_in.at[i])
+    first = 2 * p.chunk
+    r = dot3(inverse_ref[:, 0:first], w_full[0:first, :])
     landed("wb_yag", wb_in)
-    for i in range(A_CHUNKS):
+    for i in range(2, A_CHUNKS):
         landed(f"wa{i}_xag", wa_in.at[i])
-    r = dot3(inverse_ref[...], w_full[...])
+    r = r + dot3(inverse_ref[:, first:], w_full[first:, :])
     right[c] = r
     push("right_core", right.at[c], right.at[c], other)
     folded = r[:, 0:128] * r[:, 0:128]

time: 77 us -> 76.9 us (level)
  no operation moved by 1% of the time
where the time goes in v8:
time: 76.9 us; the launch traced here: 76.8 us
  Pallas kernels  76.1 us (99%)
    pallas_call x1, Pallas kernels, local_step(): pl.pallas_call(functools.partial(kernel, p), out_shape=(shaped(p.rows, p....  75 us

profile of v8, /device:TPU:1, one launch (start us, length us, event | category | flops | bytes accessed | tf_op | source)
XLA Modules:
  0.0 76.8 jit_solution(9670128300357598173)
XLA Ops:
  0.6 75.0 %dion.1 = (f32[128,1024]{1,0:T(8,128)S(1)}, f32[2,256,512]{2,1,0:T(8,128)S(1)}, f32[128,256]{1,0:T(8,128)S(1)}) custom-call(f32[128,1024]{1,0:T(8,128)} %m_hbm.1, f32[1024,256]{1,0:T(8,128)} %q_hbm.1), custom_call_target="tpu_custom_call" | custom-call | tf_op jit(solution)/shard_map/dion/pallas_call | solution.py:497
  75.6 1.2 %outputs.1 = (f32[128,1024]{1,0:T(8,128)}, f32[128,1024]{1,0:T(8,128)}) custom-call(f32[128,1024]{1,0:T(8,128)S(1)} %get-tuple-element.5.new_ref, f32[2,256,512]{2,1,0:T(8,128)S(1)} %get-tuple-element.6.right_ref, f32[128,256]{1,0:T(8,128)S(1)} %get-tuple-element.7.left_ref), custom_call_target="tpu_custom_call" | custom-call | tf_op jit(solution)/shard_map/outputs/pallas_call | solution.py:537
